TPU v7x, 32 devices: a whole 2x2x4 slice. The times are simulated.
32 devices in a mesh: expert: 16 (over z, y, x), dp: 2 (over core).
Axes of the slice: x: 2, y: 2, z: 4, core: 2. Of those that a mesh axis runs over, the one named last changes fastest.
Arguments:
- tokens: bfloat16 [4096, 3584], P('expert'), may hold values from -6 to 6
- expert_ids: int32 [4096, 8], P('expert'), may hold values from 0 to 255, all different within a row; in each aligned block of 256 rows (0 to 255, 256 to 511, ...) at most 16 rows name the same one
- gate_values: float32 [4096, 8], P('expert'), may hold values from 0.1 to 1
- tiles: int32 [16], P('expert'), may hold values from 1 to 2
- w_gate: bfloat16 [16, 3584, 2048], P('expert', None, 'dp'), may hold values from -0.09375 to 0.09375
- w_up: bfloat16 [16, 3584, 2048], P('expert', None, 'dp'), may hold values from -0.09375 to 0.09375
- w_down: bfloat16 [16, 2048, 3584], P('expert', 'dp'), may hold values from -0.125 to 0.125
- grad_out: bfloat16 [4096, 3584], P('expert', 'dp'), may hold values from -6 to 6
Outputs:
- mixed: bfloat16 [4096, 3584], P('expert', 'dp')
- grad_tokens: bfloat16 [4096, 3584], P('expert', 'dp')
- grad_gates: float32 [4096, 8], P('expert')
- grad_w_gate: bfloat16 [16, 3584, 2048], P('expert', None, 'dp')
- grad_w_up: bfloat16 [16, 3584, 2048], P('expert', None, 'dp')
- grad_w_down: bfloat16 [16, 2048, 3584], P('expert', 'dp')
Inputs may be any that keep to these rules, and one draw needn't show every extreme that they name: `expert_ids`: each row names 8 different experts. Within the rows of one device (aligned blocks of 256 rows) no expert is named by more than 16 rows.
All inputs are finite; a program needn't handle non-finite values.
Results may differ from a plain program's by a relative error of at most 0.015.
Values may be sent and summed in bfloat16 or wider, within the bound.
No kernel may reach another device: no remote copies, remote signals or barrier semaphores. Data moves between devices by JAX's collectives and lax.ppermute only.
A program may use at most 128 MiB of HBM per device.

v0:
```python
import jax
import jax.numpy as jnp
from jax import lax
from jax.sharding import PartitionSpec as P

TILE = 128
SLOTS = 16


def route_tables(ids, gates, count, experts, slots, tile):
    tok, top = ids.shape
    queue = experts * slots
    live = jnp.arange(tok, dtype=jnp.int32) < count * tile
    valid = (ids < experts) & live[:, None]
    flat_ids = ids.reshape(-1)
    flat_valid = valid.reshape(-1)
    onehot = (
        (flat_ids[:, None] == jnp.arange(experts, dtype=jnp.int32)[None, :]) & flat_valid[:, None]
    ).astype(jnp.int32)
    ranks = jnp.sum((jnp.cumsum(onehot, axis=0) - 1) * onehot, axis=1)
    target = jnp.where(flat_valid, flat_ids * slots + ranks, -1)
    match = (target[None, :] == jnp.arange(queue, dtype=jnp.int32)[:, None]).astype(jnp.float32)
    picker = jnp.sum(match.reshape(queue, tok, top), axis=2)
    slot_gate = jnp.dot(match, gates.reshape(-1), precision=lax.Precision.HIGHEST)
    return (match, picker, slot_gate)


def spread_rows(picker_tb, values):
    upper = values.astype(jnp.bfloat16)
    lower = (values - upper.astype(jnp.float32)).astype(jnp.bfloat16)
    return jnp.dot(picker_tb, upper, preferred_element_type=jnp.float32) + jnp.dot(
        picker_tb, lower, preferred_element_type=jnp.float32
    )


def on_device(tokens, expert_ids, gate_values, tiles, w_gate, w_up, w_down, grad_out):
    experts = lax.axis_size("expert")
    groups = lax.axis_size("dp")
    tok_rows, width = tokens.shape
    top = expert_ids.shape[1]
    queue = experts * SLOTS
    columns = width // groups
    match, picker, slot_gate = route_tables(expert_ids, gate_values, tiles[0], experts, SLOTS, TILE)
    pick_b = picker.astype(jnp.bfloat16)
    picker_tb = picker.T.astype(jnp.bfloat16)
    gathered = (
        jnp.dot(pick_b, tokens, preferred_element_type=jnp.float32)
        .astype(jnp.bfloat16)
        .reshape(experts, SLOTS, width)
    )
    arrived = lax.all_to_all(gathered, "expert", split_axis=0, concat_axis=0, tiled=True)
    rows = arrived.reshape(queue, width)
    w_g = w_gate[0]
    w_u = w_up[0]
    w_d = w_down[0]
    gate_pre = jnp.dot(rows, w_g, preferred_element_type=jnp.float32)
    up_pre = jnp.dot(rows, w_u, preferred_element_type=jnp.float32)
    sig = jax.nn.sigmoid(gate_pre)
    hidden = (gate_pre * sig * up_pre).astype(jnp.bfloat16)
    partial_value = jnp.dot(hidden, w_d, preferred_element_type=jnp.float32)
    summed = lax.psum_scatter(
        partial_value.reshape(experts, SLOTS, width).astype(jnp.bfloat16),
        "dp",
        scatter_dimension=2,
        tiled=True,
    ).astype(jnp.float32)
    returned = (
        lax.all_to_all(
            summed.astype(jnp.bfloat16), "expert", split_axis=0, concat_axis=0, tiled=True
        )
        .astype(summed.dtype)
        .reshape(queue, columns)
    )
    mixed = spread_rows(picker_tb, returned * slot_gate[:, None]).astype(jnp.bfloat16)
    dy_rows = jnp.dot(pick_b, grad_out, preferred_element_type=jnp.float32)
    score = lax.psum(jnp.sum(dy_rows * returned, axis=1), "dp")
    dyrow = (dy_rows * slot_gate[:, None]).astype(jnp.bfloat16).reshape(experts, SLOTS, columns)
    dy_arrived = lax.all_to_all(dyrow, "expert", split_axis=0, concat_axis=0, tiled=True)
    dy_arrived = lax.all_gather(dy_arrived, "dp", axis=2, tiled=True)
    dy_slots = dy_arrived.reshape(queue, width)
    d_hidden = jnp.dot(dy_slots, w_d.T, preferred_element_type=jnp.float32)
    d_gate = (d_hidden * up_pre * sig * (1.0 + gate_pre * (1.0 - sig))).astype(jnp.bfloat16)
    d_up = (d_hidden * gate_pre * sig).astype(jnp.bfloat16)
    grad_down = jnp.dot(hidden.T, dy_slots, preferred_element_type=jnp.float32).astype(jnp.bfloat16)
    grad_gate = jnp.dot(rows.T, d_gate, preferred_element_type=jnp.float32).astype(jnp.bfloat16)
    grad_up = jnp.dot(rows.T, d_up, preferred_element_type=jnp.float32).astype(jnp.bfloat16)
    input_rows = jnp.dot(d_gate, w_g.T, preferred_element_type=jnp.float32) + jnp.dot(
        d_up, w_u.T, preferred_element_type=jnp.float32
    )
    input_summed = lax.psum_scatter(
        input_rows.reshape(experts, SLOTS, width).astype(jnp.bfloat16),
        "dp",
        scatter_dimension=2,
        tiled=True,
    ).astype(jnp.float32)
    input_back = (
        lax.all_to_all(
            input_summed.astype(jnp.bfloat16), "expert", split_axis=0, concat_axis=0, tiled=True
        )
        .astype(input_summed.dtype)
        .reshape(queue, columns)
    )
    grad_tokens = spread_rows(picker_tb, input_back).astype(jnp.bfloat16)
    grad_gates = jnp.dot(score, match, precision=lax.Precision.HIGHEST).reshape(tok_rows, top)
    return (mixed, grad_tokens, grad_gates, grad_gate[None], grad_up[None], grad_down[None])


def solution(mesh):
    placed = (
        P("expert", None),
        P("expert", None),
        P("expert", None),
        P("expert"),
        P("expert", None, "dp"),
        P("expert", None, "dp"),
        P("expert", "dp", None),
        P("expert", "dp"),
    )
    return jax.shard_map(
        on_device,
        mesh=mesh,
        in_specs=placed,
        out_specs=(
            P("expert", "dp"),
            P("expert", "dp"),
            P("expert", None),
            P("expert", None, "dp"),
            P("expert", None, "dp"),
            P("expert", "dp", None),
        ),
        check_vma=False,
    )
```

profile of v0, /device:TPU:0, one launch (start us, length us, event | category | flops | bytes accessed | tf_op | source)
XLA Modules:
  0.0 200.1 jit_solution(2489776271005752056)
XLA Ops:
  8.0 0.7 compare_and_fusion
  8.8 0.2 copy.33
  8.9 0.1 and.28
  9.1 0.1 and.31
  9.2 0.8 copy.32
  10.0 0.1 eq.45
  10.1 0.1 eq.49
  10.3 4.5 %reduce-window.6 = s32[16,16,128]{2,1,0:T(8,128)S(1)} reduce-window(s32[16,16,128]{2,1,0:T(8,128)S(1)} %fusion.40, s32[]{:T(128)} %constant.8.clone.1), window={size=1x1x128 pad=0_0x0_0x127_0}, to_apply=%region_0.0 | reduce-window | flops 4161536 | bytes 262148 | tf_op jit(solution)/shard_map/reduce-window
  14.8 0.4 slice_reduce_fusion
  15.2 0.2 reduce-window.9
  15.4 0.1 add_add_fusion
  15.6 0.1 reduce_sum.30
  15.8 0.9 convert_reduce_fusion
  16.7 0.1 copy.37
  16.8 0.1 reshape.117
  16.9 1.0 fusion.29
  17.9 2.0 multiply_convert_fusion
  19.9 8.3 %all-to-all-start.2 = ((bf16[16,16,1792]{2,1,0:T(8,128)(2,1)}), bf16[16,16,1792]{2,1,0:T(8,128)(2,1)S(1)}, u32[]{:S(2)}, u32[]{:S(2)}) async-start(bf16[16,16,1792]{2,1,0:T(8,128)(2,1)} %bitcast.89), calls=%async_computation.3 | async-start | bytes 1835008 | tf_op jit(solution)/shard_map/all_to_all | solution.py:78
  28.3 1.9 convolution_convert_fusion.3
  30.1 20.1 %all-to-all-done.2 = bf16[16,16,1792]{2,1,0:T(8,128)(2,1)S(1)} async-done(((bf16[16,16,1792]{2,1,0:T(8,128)(2,1)}), bf16[16,16,1792]{2,1,0:T(8,128)(2,1)S(1)}, u32[]{:S(2)}, u32[]{:S(2)}) %all-to-all-start.2) | async-done | bytes 917536 | tf_op jit(solution)/shard_map/all_to_all | solution.py:78
  50.2 0.9 copy-done.6
  51.2 5.5 %all-to-all-start = ((bf16[16,16,3584]{2,1,0:T(8,128)(2,1)}), bf16[16,16,3584]{2,1,0:T(8,128)(2,1)S(1)}, u32[]{:S(2)}, u32[]{:S(2)}) async-start(bf16[16,16,3584]{2,1,0:T(8,128)(2,1)} %bitcast.88), calls=%async_computation | async-start | bytes 3670016 | tf_op jit(solution)/shard_map/all_to_all | solution.py:51
  56.7 0.7 all-gather.2.cloned.1.call-update
  57.4 36.8 %all-to-all-done = bf16[16,16,3584]{2,1,0:T(8,128)(2,1)S(1)} async-done(((bf16[16,16,3584]{2,1,0:T(8,128)(2,1)}), bf16[16,16,3584]{2,1,0:T(8,128)(2,1)S(1)}, u32[]{:S(2)}, u32[]{:S(2)}) %all-to-all-start) | async-done | bytes 1835040 | tf_op jit(solution)/shard_map/all_to_all | solution.py:51
  94.2 6.1 %fusion.6 = f32[256,1024]{1,0:T(8,128)} fusion(bf16[256,3584]{1,0:T(8,128)(2,1)S(1)} %bitcast.83, bf16[1,3584,1024]{2,1,0:T(8,128)(2,1)} %param.13), kind=kOutput, calls=%fused_computation.9 | convolution fusion | flops 1879048192 | bytes 10223616 | tf_op jit(solution)/shard_map/dot_general | solution.py:57
  100.3 5.9 %fusion.2 = f32[256,1024]{1,0:T(8,128)S(1)} fusion(bf16[256,3584]{1,0:T(8,128)(2,1)} %bitcast.90, bf16[1,1024,3584]{2,1,0:T(8,128)(2,1)} %param.14), kind=kOutput, calls=%fused_computation.5 | convolution fusion | flops 1879048192 | bytes 10223616 | tf_op jit(solution)/shard_map/dot_general | solution.py:81
  106.2 6.6 %multiply_convert_fusion.2 = (bf16[256,1024]{1,0:T(8,128)(2,1)}, bf16[256,1024]{1,0:T(8,128)(2,1)S(1)}, bf16[256,1024]{1,0:T(8,128)(2,1)S(1)}) fusion(f32[256,1024]{1,0:T(8,128)S(1)} %fusion.2, f32[256,1024]{1,0:T(8,128)S(1)} %copy-done.14, bf16[256,3584]{1,0:T(8,128)(2,1)S(1)} %bitcast.84, bf16[1,3584,1024]{2,1,0:T(8,128)(2,1)} %param.12), kind=kOutput, calls=%fused_computation.40 | convolution fusion | flops 1883242496 | bytes 12845056 | tf_op jit(solution)/shard_map/dot_general | solution.py:56
  112.8 3.3 %fusion.18 = bf16[16,16,3584]{2,1,0:T(8,128)(2,1)} fusion(bf16[16,16,1024]{2,1,0:T(8,128)(2,1)S(1)} %bitcast.93, bf16[1,1024,3584]{2,1,0:T(8,128)(2,1)S(1)} %bitcast.102), kind=kOutput, calls=%fused_computation.19 | convolution fusion | flops 1879965696 | bytes 9699328 | tf_op jit(solution)/shard_map/dot_general | solution.py:60
  116.1 0.2 reduce-scatter.5.cloned.1.call-start
  116.4 5.2 %fusion.4 = f32[256,3584]{1,0:T(8,128)S(1)} fusion(bf16[256,1024]{1,0:T(8,128)(2,1)S(1)} %get-tuple-element.26, bf16[1,3584,1024]{2,1,0:T(8,128)(2,1)} %param.13), kind=kOutput, calls=%fused_computation.7 | convolution fusion | flops 1879048192 | bytes 11534336 | tf_op jit(solution)/shard_map/dot_general | solution.py:87
  121.6 6.5 %fusion.21 = bf16[256,3584]{1,0:T(8,128)(2,1)} fusion(f32[256,3584]{1,0:T(8,128)S(1)} %fusion.4, bf16[256,1024]{1,0:T(8,128)(2,1)S(1)} %copy-done.10, bf16[1,3584,1024]{2,1,0:T(8,128)(2,1)} %param.12), kind=kOutput, calls=%fused_computation.21 | convolution fusion | flops 1880883200 | bytes 13369344 | tf_op jit(solution)/shard_map/dot_general | solution.py:87
  128.1 0.4 reduce-scatter.3.cloned.1.call-done
  128.5 8.9 %all-to-all-start.1 = ((bf16[16,16,1792]{2,1,0:T(8,128)(2,1)}), bf16[16,16,1792]{2,1,0:T(8,128)(2,1)S(1)}, u32[]{:S(2)}, u32[]{:S(2)}) async-start(bf16[16,16,1792]{2,1,0:T(8,128)(2,1)} %reduce-scatter.3.cloned.1.call-done), calls=%async_computation.2 | async-start | bytes 1835008 | tf_op jit(solution)/shard_map/all_to_all | solution.py:68
  137.4 4.5 %reduce-scatter.5.cloned.1.call-done = bf16[16,16,1792]{2,1,0:T(8,128)(2,1)} async-done(((bf16[16,16,3584]{2,1,0:T(8,128)(2,1)}), bf16[16,16,1792]{2,1,0:T(8,128)(2,1)}) %reduce-scatter.5.cloned.1.call-update) | async-done | bytes 917520 | tf_op jit(solution)/shard_map/reduce_scatter | solution.py:90
  142.0 16.7 %all-to-all-done.1 = bf16[16,16,1792]{2,1,0:T(8,128)(2,1)S(1)} async-done(((bf16[16,16,1792]{2,1,0:T(8,128)(2,1)}), bf16[16,16,1792]{2,1,0:T(8,128)(2,1)S(1)}, u32[]{:S(2)}, u32[]{:S(2)}) %all-to-all-start.1) | async-done | bytes 917536 | tf_op jit(solution)/shard_map/all_to_all | solution.py:68
  158.7 5.5 %all-to-all-start.3 = ((bf16[16,16,1792]{2,1,0:T(8,128)(2,1)}), bf16[16,16,1792]{2,1,0:T(8,128)(2,1)}, u32[]{:S(2)}, u32[]{:S(2)}) async-start(bf16[16,16,1792]{2,1,0:T(8,128)(2,1)} %reduce-scatter.5.cloned.1.call-done), calls=%async_computation.5 | async-start | bytes 1835008 | tf_op jit(solution)/shard_map/all_to_all | solution.py:97
  164.2 6.7 %fusion.14 = bf16[1,1024,3584]{2,1,0:T(8,128)(2,1)} fusion(bf16[256,1024]{1,0:T(8,128)(2,1)S(1)} %get-tuple-element.25, bf16[256,3584]{1,0:T(8,128)(2,1)} %bitcast.91), kind=kOutput, calls=%fused_computation.17 | convolution fusion | flops 1882718208 | bytes 9699328 | tf_op jit(solution)/shard_map/dot_general | solution.py:84
  171.0 5.2 %fusion.12 = bf16[1,3584,1024]{2,1,0:T(8,128)(2,1)} fusion(bf16[256,3584]{1,0:T(8,128)(2,1)S(1)} %bitcast.85, bf16[256,1024]{1,0:T(8,128)(2,1)S(1)} %copy-done.11), kind=kOutput, calls=%fused_computation.15 | convolution fusion | flops 1882718208 | bytes 9699328 | tf_op jit(solution)/shard_map/dot_general | solution.py:85
  176.1 5.2 %fusion.13 = bf16[1,3584,1024]{2,1,0:T(8,128)(2,1)} fusion(bf16[256,3584]{1,0:T(8,128)(2,1)S(1)} %bitcast.86, bf16[256,1024]{1,0:T(8,128)(2,1)S(1)} %copy-done.9), kind=kOutput, calls=%fused_computation.16 | convolution fusion | flops 1882718208 | bytes 9699328 | tf_op jit(solution)/shard_map/dot_general | solution.py:86
  181.3 0.4 fusion.31
  181.7 2.7 %psum.7 = f32[256]{0:T(256)S(1)} all-reduce(f32[256]{0:T(256)S(1)} %get-tuple-element.27), channel_id=1, replica_groups=mesh['expert'=16,'dp'=2] {'dp'}, use_global_device_ids=true, to_apply=%region_7.8 | all-reduce | flops 256 | bytes 2048 | tf_op jit(solution)/shard_map/psum | solution.py:76
  184.4 0.8 fusion.28
  185.2 0.1 reshape.113
  185.3 0.7 copy.38
  185.9 1.7 fusion.41
  187.6 1.6 fusion.42
  189.3 2.7 %fusion.25 = bf16[256,1792]{1,0:T(8,128)(2,1)} fusion(f32[256,1792]{1,0:T(8,128)S(1)} %fusion.42, bf16[256,256]{1,0:T(8,128)(2,1)S(1)} %convert_reduce_fusion, bf16[256,1792]{1,0:T(8,128)(2,1)} %bitcast.14), kind=kOutput, calls=%fused_computation.25 | convolution fusion | flops 237174784 | bytes 3801088 | tf_op jit(solution)/shard_map/dot_general | solution.py:31
  192.0 1.5 fusion.24
  (46 shorter events, 0.4 us)
Async XLA Ops:
  7.2 21.1 %copy-start = (bf16[256,3584]{1,0:T(8,128)(2,1)S(1)}, bf16[256,3584]{1,0:T(8,128)(2,1)}, u32[]{:S(2)}) copy-start(bf16[256,3584]{1,0:T(8,128)(2,1)} %param.8) | copy-start | bytes 5505028
  7.2 8.6 %copy-start.12 = (s32[256,8]{0,1:T(8,128)S(1)}, s32[256,8]{0,1:T(8,128)}, u32[]{:S(2)}) copy-start(s32[256,8]{0,1:T(8,128)} %param.9) | copy-start | bytes 24580
  7.2 9.5 %copy-start.13 = (f32[256,8]{0,1:T(8,128)S(1)}, f32[256,8]{0,1:T(8,128)}, u32[]{:S(2)}) copy-start(f32[256,8]{0,1:T(8,128)} %param.10) | copy-start | bytes 24580
  7.2 10.7 %copy-start.7 = (bf16[256,1792]{1,0:T(8,128)(2,1)S(1)}, bf16[256,1792]{1,0:T(8,128)(2,1)}, u32[]{:S(2)}) copy-start(bf16[256,1792]{1,0:T(8,128)(2,1)} %param.15) | copy-start | bytes 2752516
  19.9 30.3 %all-to-all-start.2 = ((bf16[16,16,1792]{2,1,0:T(8,128)(2,1)}), bf16[16,16,1792]{2,1,0:T(8,128)(2,1)S(1)}, u32[]{:S(2)}, u32[]{:S(2)}) async-start(bf16[16,16,1792]{2,1,0:T(8,128)(2,1)} %bitcast.89), calls=%async_computation.3 | async-start | bytes 1835008 | tf_op jit(solution)/shard_map/all_to_all | solution.py:78
  50.2 0.9 copy-start.6
  51.2 43.0 %all-to-all-start = ((bf16[16,16,3584]{2,1,0:T(8,128)(2,1)}), bf16[16,16,3584]{2,1,0:T(8,128)(2,1)S(1)}, u32[]{:S(2)}, u32[]{:S(2)}) async-start(bf16[16,16,3584]{2,1,0:T(8,128)(2,1)} %bitcast.88), calls=%async_computation | async-start | bytes 3670016 | tf_op jit(solution)/shard_map/all_to_all | solution.py:51
  56.6 43.7 %all-gather.2.cloned.1.call-start = ((), (), s32[]{:S(2)}) async-start(), calls=%async_computation.7 | async-start | bytes 2752512 | tf_op jit(solution)/shard_map/all_gather | solution.py:79
  57.4 71.1 %reduce-scatter.3.cloned.1.call-start = ((), (), s32[]{:S(2)}) async-start(), calls=%async_computation.6 | async-start | bytes 2752512 | tf_op jit(solution)/shard_map/reduce_scatter | solution.py:61
  100.3 5.9 %copy-start.14 = (f32[256,1024]{1,0:T(8,128)S(1)}, f32[256,1024]{1,0:T(8,128)}, u32[]{:S(2)}) copy-start(f32[256,1024]{1,0:T(8,128)} %fusion.6) | copy-start | bytes 3145732
  100.3 12.5 %slice-start = ((s8[7340032]{0:T(1024)(128)(4,1)}), s8[3145728]{0:T(1024)(128)(4,1)S(1)}, s32[]{:S(2)}) async-start(s8[7340032]{0:T(1024)(128)(4,1)} %bitcast.101), calls=%async_computation.9 | async-start | bytes 6291456
  106.2 6.6 %slice-start.1 = ((s8[7340032]{0:T(1024)(128)(4,1)}), s8[4194304]{0:T(1024)(128)(4,1)S(1)}, s32[]{:S(2)}) async-start(s8[7340032]{0:T(1024)(128)(4,1)} %bitcast.101), calls=%async_computation.10 | async-start | bytes 8388608
  112.8 3.6 %copy-start.8 = (bf16[256,1024]{1,0:T(8,128)(2,1)}, bf16[256,1024]{1,0:T(8,128)(2,1)S(1)}, u32[]{:S(2)}) copy-start(bf16[256,1024]{1,0:T(8,128)(2,1)S(1)} %get-tuple-element.26) | copy-start | bytes 1572868
  116.1 25.8 %reduce-scatter.5.cloned.1.call-start = ((), (), s32[]{:S(2)}) async-start(), calls=%async_computation.8 | async-start | bytes 2752512 | tf_op jit(solution)/shard_map/reduce_scatter | solution.py:90
  116.4 5.3 %copy-start.10 = (bf16[256,1024]{1,0:T(8,128)(2,1)S(1)}, bf16[256,1024]{1,0:T(8,128)(2,1)}, u32[]{:S(2)}) copy-start(bf16[256,1024]{1,0:T(8,128)(2,1)} %get-tuple-element.24) | copy-start | bytes 1572868
  128.5 30.2 %all-to-all-start.1 = ((bf16[16,16,1792]{2,1,0:T(8,128)(2,1)}), bf16[16,16,1792]{2,1,0:T(8,128)(2,1)S(1)}, u32[]{:S(2)}, u32[]{:S(2)}) async-start(bf16[16,16,1792]{2,1,0:T(8,128)(2,1)} %reduce-scatter.3.cloned.1.call-done), calls=%async_computation.2 | async-start | bytes 1835008 | tf_op jit(solution)/shard_map/all_to_all | solution.py:68
  158.7 29.0 %all-to-all-start.3 = ((bf16[16,16,1792]{2,1,0:T(8,128)(2,1)}), bf16[16,16,1792]{2,1,0:T(8,128)(2,1)}, u32[]{:S(2)}, u32[]{:S(2)}) async-start(bf16[16,16,1792]{2,1,0:T(8,128)(2,1)} %reduce-scatter.5.cloned.1.call-done), calls=%async_computation.5 | async-start | bytes 1835008 | tf_op jit(solution)/shard_map/all_to_all | solution.py:97
  164.2 6.7 %copy-start.11 = (bf16[256,1024]{1,0:T(8,128)(2,1)S(1)}, bf16[256,1024]{1,0:T(8,128)(2,1)}, u32[]{:S(2)}) copy-start(bf16[256,1024]{1,0:T(8,128)(2,1)} %get-tuple-element.24) | copy-start | bytes 1572868
  171.0 5.2 %copy-start.9 = (bf16[256,1024]{1,0:T(8,128)(2,1)S(1)}, bf16[256,1024]{1,0:T(8,128)(2,1)}, u32[]{:S(2)}) copy-start(bf16[256,1024]{1,0:T(8,128)(2,1)} %copy-done.8) | copy-start | bytes 1572868
  176.1 5.2 %copy-start.5 = (f32[256,1792]{1,0:T(8,128)S(1)}, f32[256,1792]{1,0:T(8,128)}, u32[]{:S(2)}) copy-start(f32[256,1792]{1,0:T(8,128)} %get-tuple-element.30) | copy-start | bytes 5505028
  181.7 5.9 %copy-start.2 = (bf16[256,1792]{1,0:T(8,128)(2,1)}, bf16[256,1792]{1,0:T(8,128)(2,1)S(1)}, u32[]{:S(2)}) copy-start(bf16[256,1792]{1,0:T(8,128)(2,1)S(1)} %get-tuple-element.28) | copy-start | bytes 2752516
  189.3 2.7 %copy-start.3 = (bf16[256,1792]{1,0:T(8,128)(2,1)S(1)}, bf16[256,1792]{1,0:T(8,128)(2,1)}, u32[]{:S(2)}) copy-start(bf16[256,1792]{1,0:T(8,128)(2,1)} %copy-done.2) | copy-start | bytes 2752516
  189.3 2.7 %copy-start.4 = (f32[256,1792]{1,0:T(8,128)S(1)}, f32[256,1792]{1,0:T(8,128)}, u32[]{:S(2)}) copy-start(f32[256,1792]{1,0:T(8,128)} %fusion.41) | copy-start | bytes 5505028
  192.0 1.5 copy-start.1
Sparse Core Ops, SparseCore 0:
  59.6 11.4 all-gather.1
  116.2 12.2 reduce-scatter.2
  131.3 10.5 reduce-scatter.4
where the time goes:
time: 201 us; the launch traced here: 200 us
  waiting for transfers between devices  79.2 us (39%)
  matrix products  63.7 us (32%)
  starting transfers between devices  28.5 us (14%)
  between operations  14.8 us (7%)
  other arithmetic  6.98 us (3%)
  local copies, waits for them, and re-layouts  4.05 us (2%)
  blocking collectives  2.69 us (1%)
    all_to_all x1, waiting for transfers between devices, on_device(): lax.all_to_all(gathered, 'expert', split_axis=0, concat_axis=0, tiled=True)  36.8 us
    all_to_all x1, waiting for transfers between devices, on_device(): lax.all_to_all(dyrow, 'expert', split_axis=0, concat_axis=0, tiled=True)  20.1 us
    all_to_all x1, waiting for transfers between devices, on_device(): lax.all_to_all(summed.astype(jnp.bfloat16), 'expert', split_axis=0, conca...  16.7 us
    all_to_all x1, starting transfers between devices, on_device(): lax.all_to_all(summed.astype(jnp.bfloat16), 'expert', split_axis=0, conca...  8.89 us
    all_to_all x1, starting transfers between devices, on_device(): lax.all_to_all(dyrow, 'expert', split_axis=0, concat_axis=0, tiled=True)  8.34 us
    dot_general x1, matrix products, on_device(): jnp.dot(hidden.T, dy_slots, preferred_element_type=jnp.float32)  6.72 us
    dot_general x1, matrix products, on_device(): gate_pre = jnp.dot(rows, w_g, preferred_element_type=jnp.float32)  6.56 us
    dot_general x1, matrix products, on_device(): jnp.dot(d_gate, w_g.T, preferred_element_type=jnp.float32)  6.49 us
  transfers between devices with their start and end apart: 7, of which 5 were waited for; matrix products, arithmetic and copies ran while one was open for 20% of the time, Pallas kernels for 0%

commit v1 on v0

v1 whole, which is shorter than its diff:
```python
import functools
import math

import jax
import jax.numpy as jnp
from jax import lax
from jax.experimental import pallas as pl
from jax.experimental.pallas import tpu as pltpu
from jax.sharding import PartitionSpec as P


TILE = 128
SLOTS = 16
F32 = jnp.float32
BF16 = jnp.bfloat16
VMEM = pl.BlockSpec(memory_space=pltpu.VMEM)
ANY = pl.BlockSpec(memory_space=pl.ANY)
SMEM = pl.BlockSpec(memory_space=pltpu.SMEM)
STEP = 256
PARTS = 4
DMAS = pltpu.SemaphoreType.DMA((PARTS,))


def params(mib):
    return pltpu.CompilerParams(vmem_limit_bytes=mib << 20)


def cost(flops, moved):
    return pl.CostEstimate(flops=flops, bytes_accessed=moved, transcendentals=0)


def dot_nn(a, b):
    return jnp.dot(a, b, preferred_element_type=F32)


def dot_nt(a, b):
    return lax.dot_general(a, b, (((1,), (1,)), ((), ())), preferred_element_type=F32)


def dot_tn(a, b):
    return lax.dot_general(a, b, (((0,), (0,)), ((), ())), preferred_element_type=F32)


def dispatch_kernel(where_ref, ids_ref, gates_ref, tok_ref, send_ref, pick_ref, weight_ref):
    top, tok = ids_ref.shape
    queue = pick_ref.shape[0]
    owner = lax.broadcasted_iota(jnp.int32, (queue, tok), 0)
    expert, slot = owner // SLOTS, owner % SLOTS
    ids, gates = ids_ref[...], gates_ref[...]
    named = jnp.zeros((queue, tok), F32)
    weight = jnp.zeros((queue, tok), F32)
    for k in range(top):
        hit = jnp.broadcast_to(ids[k : k + 1, :], (queue, tok)) == expert
        named = jnp.where(hit, 1.0, named)
        weight = jnp.where(hit, jnp.broadcast_to(gates[k : k + 1, :], (queue, tok)), weight)
    live = lax.broadcasted_iota(jnp.int32, (queue, tok), 1) < where_ref[1] * TILE
    named = jnp.where(live, named, 0.0)
    before = lax.broadcasted_iota(jnp.int32, (tok, tok), 0) < lax.broadcasted_iota(
        jnp.int32, (tok, tok), 1
    )
    rank = dot_nn(named.astype(BF16), jnp.where(before, 1.0, 0.0).astype(BF16))
    chosen = (named > 0.5) & (rank == slot.astype(F32))
    pick = jnp.where(chosen, 1.0, 0.0).astype(BF16)
    send_ref[...] = dot_nn(pick, tok_ref[...]).astype(BF16)
    pick_ref[...] = pick
    weight_ref[...] = jnp.where(chosen, weight, 0.0)


def cotangent_kernel(pick_ref, weight_ref, out_ref, send_ref):
    gate = jnp.sum(weight_ref[...], axis=1, keepdims=True)
    send_ref[...] = (dot_nn(pick_ref[...], out_ref[...]) * gate).astype(BF16)


def combine_kernel(pick_ref, weight_ref, ids_ref, back_ref, out_ref, mixed_ref, score_ref):
    back = back_ref[...]
    weight = weight_ref[...]
    upper = weight.astype(BF16)
    lower = (weight - upper.astype(F32)).astype(BF16)
    mixed_ref[...] = (dot_tn(upper, back) + dot_tn(lower, back)).astype(BF16)
    pairs = dot_nt(back, out_ref[...])
    pairs = jnp.where(pick_ref[...] > 0.5, pairs, 0.0)
    queue, tok = pairs.shape
    expert = lax.broadcasted_iota(jnp.int32, (queue, tok), 0) // SLOTS
    ids = ids_ref[...]
    for k in range(ids.shape[0]):
        hit = jnp.broadcast_to(ids[k : k + 1, :], (queue, tok)) == expert
        score_ref[k : k + 1, :] = jnp.sum(jnp.where(hit, pairs, 0.0), axis=0, keepdims=True)


def spread_kernel(pick_ref, back_ref, out_ref):
    out_ref[...] = dot_tn(pick_ref[...], back_ref[...]).astype(BF16)


def fetch(src, dst, sems):
    rows = src.shape[0] // PARTS
    return [
        pltpu.make_async_copy(src.at[pl.ds(i * rows, rows)], dst.at[pl.ds(i * rows, rows)], sems.at[i])
        for i in range(PARTS)
    ]


def begin(copies):
    for copy in copies:
        copy.start()


def finish(copies):
    for copy in copies:
        copy.wait()


def load_kernel(*refs):
    n = len(refs) // 3
    copies = []
    for src, dst, sems in zip(refs[:n], refs[n : 2 * n], refs[2 * n :]):
        copies += fetch(src, dst, sems)
    begin(copies)
    finish(copies)


def enter_kernel(part_ref, x_ref, wg_ref, wu_ref, next_ref, g_ref, u_ref, kept_ref, sems):
    copies = fetch(next_ref, kept_ref, sems)
    begin(copies)
    k = x_ref.shape[1]
    first = pl.multiple_of(part_ref[0] * k, 128)
    for j in range(0, g_ref.shape[1], STEP):
        c = slice(j, j + STEP)
        g_ref[:, c] = dot_nn(x_ref[...], wg_ref[pl.ds(first, k), c])
        u_ref[:, c] = dot_nn(x_ref[...], wu_ref[pl.ds(first, k), c])
    finish(copies)


def hidden_kernel(part_ref, x_ref, wg_ref, wu_ref, g0_ref, u0_ref, h_ref, a_ref, b_ref):
    k = x_ref.shape[1]
    first = pl.multiple_of(part_ref[0] * k, 128)
    for j in range(0, h_ref.shape[1], STEP):
        c = slice(j, j + STEP)
        g = g0_ref[:, c] + dot_nn(x_ref[...], wg_ref[pl.ds(first, k), c])
        u = u0_ref[:, c] + dot_nn(x_ref[...], wu_ref[pl.ds(first, k), c])
        sig = jax.nn.sigmoid(g)
        gated = g * sig
        h_ref[:, c] = (gated * u).astype(BF16)
        a_ref[:, c] = (u * sig * (1.0 + g * (1.0 - sig))).astype(BF16)
        b_ref[:, c] = gated.astype(BF16)


def leave_kernel(part_ref, h_ref, w_ref, y_ref):
    n = y_ref.shape[1]
    first = part_ref[0] * n
    for j in range(0, n, STEP):
        cols = pl.ds(pl.multiple_of(first + j, 128), STEP)
        y_ref[:, j : j + STEP] = dot_nn(h_ref[...], w_ref[:, cols]).astype(y_ref.dtype)


def back_kernel(part_ref, dy_ref, w_ref, ng_ref, nu_ref, dh_ref, kg_ref, ku_ref, g_sems, u_sems):
    copies = fetch(ng_ref, kg_ref, g_sems) + fetch(nu_ref, ku_ref, u_sems)
    begin(copies)
    k = dy_ref.shape[1]
    cols = pl.ds(pl.multiple_of(part_ref[0] * k, 128), k)
    for j in range(0, dh_ref.shape[1], STEP):
        dh_ref[:, j : j + STEP] = dot_nt(dy_ref[...], w_ref[j : j + STEP, cols])
    finish(copies)


def inner_kernel(part_ref, dy_ref, w_ref, dh0_ref, a_ref, b_ref, dg_ref, du_ref):
    k = dy_ref.shape[1]
    cols = pl.ds(pl.multiple_of(part_ref[0] * k, 128), k)
    for j in range(0, dg_ref.shape[1], STEP):
        c = slice(j, j + STEP)
        dh = dh0_ref[:, c] + dot_nt(dy_ref[...], w_ref[c, cols])
        dg_ref[:, c] = (dh * a_ref[:, c].astype(F32)).astype(BF16)
        du_ref[:, c] = (dh * b_ref[:, c].astype(F32)).astype(BF16)


def input_kernel(part_ref, dg_ref, du_ref, wg_ref, wu_ref, dx_ref):
    n = dx_ref.shape[1]
    first = part_ref[0] * n
    for j in range(0, n, STEP):
        rows = pl.ds(pl.multiple_of(first + j, 128), STEP)
        dx_ref[:, j : j + STEP] = (
            dot_nt(dg_ref[...], wg_ref[rows, :]) + dot_nt(du_ref[...], wu_ref[rows, :])
        ).astype(dx_ref.dtype)


def in_hbm(x):
    return pltpu.with_memory_space_constraint(x, pltpu.HBM)


def call(kernel, outs, *args, specs=None, scratch=(), flops=0, mib=6):
    shapes = [(pltpu.VMEM if kept else jax.ShapeDtypeStruct)(s, d) for s, d, kept in outs]
    moved = sum(a.size * a.dtype.itemsize for a in args) + sum(
        math.prod(s) * jnp.dtype(d).itemsize for s, d, _ in outs
    )
    result = pl.pallas_call(
        kernel,
        in_specs=specs or [SMEM] + [VMEM] * (len(args) - 1),
        out_specs=[VMEM] * len(shapes),
        out_shape=shapes,
        scratch_shapes=list(scratch),
        compiler_params=params(mib),
        cost_estimate=cost(flops, moved),
    )(*args)
    return result if len(shapes) > 1 else result[0]


def load(*arrays):
    kept = call(
        load_kernel, [(a.shape, a.dtype, True) for a in arrays], *arrays,
        specs=[ANY] * len(arrays), scratch=[DMAS] * len(arrays),
    )
    return kept


def swap(x):
    return lax.ppermute(x, "dp", [(0, 1), (1, 0)])


def exchange(x, experts):
    rows, width = x.shape
    x = lax.all_to_all(
        x.reshape(experts, rows // experts, width), "expert", 0, 0, tiled=True
    )
    return x.reshape(rows, width)


def paired(tokens, expert_ids, gate_values, tiles, w_gate, w_up, w_down, grad_out):
    experts = lax.axis_size("expert")
    tok, width = tokens.shape
    top = expert_ids.shape[1]
    queue = experts * SLOTS
    half = width // 2
    wg, wu, wd = (in_hbm(w[0]) for w in (w_gate, w_up, w_down))
    hid = wg.shape[1]
    me = lax.axis_index("dp").astype(jnp.int32)
    mine = me.reshape(1)
    other = 1 - mine
    ids_t, gates_t = expert_ids.T, gate_values.T
    unit = 2 * queue * half * hid

    send, pick, weight = pl.pallas_call(
        dispatch_kernel,
        grid_spec=pltpu.PrefetchScalarGridSpec(
            num_scalar_prefetch=1,
            grid=(1,),
            in_specs=[
                pl.BlockSpec((top, tok), lambda i, s: (0, 0)),
                pl.BlockSpec((top, tok), lambda i, s: (0, 0)),
                pl.BlockSpec((tok, half), lambda i, s: (0, s[0])),
            ],
            out_specs=[
                pl.BlockSpec((queue, half), lambda i, s: (0, 0)),
                pl.BlockSpec((queue, tok), lambda i, s: (0, 0)),
                pl.BlockSpec((queue, tok), lambda i, s: (0, 0)),
            ],
        ),
        out_shape=[
            jax.ShapeDtypeStruct((queue, half), BF16),
            jax.ShapeDtypeStruct((queue, tok), BF16),
            jax.ShapeDtypeStruct((queue, tok), F32),
        ],
        compiler_params=params(8),
        name="dispatch",
    )(jnp.concatenate([mine, tiles]), in_hbm(ids_t), in_hbm(gates_t), in_hbm(tokens))
    x_own = exchange(send, experts)
    dy_send = call(
        cotangent_kernel, [((queue, half), BF16, False)], pick, weight, grad_out,
        specs=[VMEM] * 3, flops=2 * queue * tok * half,
    )
    dy_send, x_own = lax.optimization_barrier((dy_send, x_own))
    dy_own = exchange(dy_send, experts)

    inner = ((queue, hid), F32, True)
    x_oth = swap(x_own)
    wg0, wu0 = load(wg, wu)
    g0, u0, wd0 = call(
        enter_kernel, [inner, inner, (wd.shape, BF16, True)], mine, x_own, wg0, wu0, wd,
        specs=[SMEM] + [VMEM] * 3 + [ANY], scratch=[DMAS], flops=2 * unit,
    )
    h, a, b = call(
        hidden_kernel, [((queue, hid), BF16, False)] * 3, other, x_oth, wg0, wu0, g0, u0,
        flops=2 * unit,
    )
    y_far = call(leave_kernel, [((queue, half), BF16, False)], other, h, wd0, flops=unit)
    y_far = swap(y_far)
    y_near = call(leave_kernel, [((queue, half), F32, False)], mine, h, wd0, flops=unit)
    y_sum = (y_near + y_far.astype(F32)).astype(BF16)
    y_back = exchange(y_sum, experts)

    dy_oth = swap(dy_own)
    wd1 = load(wd)
    dh0, wg1, wu1 = call(
        back_kernel, [inner, (wg.shape, BF16, True), (wu.shape, BF16, True)], mine, dy_own, wd1, wg, wu,
        specs=[SMEM] + [VMEM] * 2 + [ANY] * 2, scratch=[DMAS] * 2, flops=unit,
    )
    dg, du = call(
        inner_kernel, [((queue, hid), BF16, False)] * 2, other, dy_oth, wd1, dh0, a, b,
        flops=unit,
    )
    dx_far = call(
        input_kernel, [((queue, half), BF16, False)], other, dg, du, wg1, wu1, flops=2 * unit
    )
    dx_far = swap(dx_far)
    dx_near = call(
        input_kernel, [((queue, half), F32, False)], mine, dg, du, wg1, wu1, flops=2 * unit
    )
    dx_sum = (dx_near + dx_far.astype(F32)).astype(BF16)
    dx_back = exchange(dx_sum, experts)

    first = me == 0
    x_full = jnp.where(
        first, jnp.concatenate([x_own, x_oth], 1), jnp.concatenate([x_oth, x_own], 1)
    )
    dy_full = jnp.where(
        first, jnp.concatenate([dy_own, dy_oth], 1), jnp.concatenate([dy_oth, dy_own], 1)
    )
    grad_down = dot_tn(h, dy_full).astype(BF16)
    grad_gate = dot_tn(x_full, dg).astype(BF16)
    grad_up = dot_tn(x_full, du).astype(BF16)

    mixed, score = call(
        combine_kernel, [((tok, half), BF16, False), ((top, tok), F32, False)],
        pick, weight, ids_t, y_back, grad_out,
        specs=[VMEM] * 5, flops=6 * queue * tok * half,
    )
    grad_gates = (score + swap(score)).T
    grad_tokens = call(
        spread_kernel, [((tok, half), BF16, False)], pick, dx_back,
        specs=[VMEM] * 2, flops=2 * queue * tok * half,
    )
    return mixed, grad_tokens, grad_gates, grad_gate[None], grad_up[None], grad_down[None]


def route_tables(ids, gates, count, experts, slots, tile):
    tok, top = ids.shape
    queue = experts * slots
    live = jnp.arange(tok, dtype=jnp.int32) < count * tile
    valid = (ids < experts) & live[:, None]
    flat_ids = ids.reshape(-1)
    flat_valid = valid.reshape(-1)
    onehot = (
        (flat_ids[:, None] == jnp.arange(experts, dtype=jnp.int32)[None, :]) & flat_valid[:, None]
    ).astype(jnp.int32)
    ranks = jnp.sum((jnp.cumsum(onehot, axis=0) - 1) * onehot, axis=1)
    target = jnp.where(flat_valid, flat_ids * slots + ranks, -1)
    match = (target[None, :] == jnp.arange(queue, dtype=jnp.int32)[:, None]).astype(F32)
    picker = jnp.sum(match.reshape(queue, tok, top), axis=2)
    slot_gate = jnp.dot(match, gates.reshape(-1), precision=lax.Precision.HIGHEST)
    return match, picker, slot_gate


def spread_rows(picker_tb, values):
    upper = values.astype(BF16)
    lower = (values - upper.astype(F32)).astype(BF16)
    return dot_nn(picker_tb, upper) + dot_nn(picker_tb, lower)


def shared(tokens, expert_ids, gate_values, tiles, w_gate, w_up, w_down, grad_out):
    experts = lax.axis_size("expert")
    groups = lax.axis_size("dp")
    tok, width = tokens.shape
    top = expert_ids.shape[1]
    columns = width // groups
    match, picker, slot_gate = route_tables(expert_ids, gate_values, tiles[0], experts, SLOTS, TILE)
    pick_b = picker.astype(BF16)
    picker_tb = picker.T.astype(BF16)
    mine = lax.dynamic_slice_in_dim(tokens, lax.axis_index("dp") * columns, columns, 1)
    rows = exchange(dot_nn(pick_b, mine).astype(BF16), experts)
    rows = lax.all_gather(rows, "dp", axis=1, tiled=True)
    w_g, w_u, w_d = w_gate[0], w_up[0], w_down[0]
    gate_pre = dot_nn(rows, w_g)
    up_pre = dot_nn(rows, w_u)
    sig = jax.nn.sigmoid(gate_pre)
    hidden = (gate_pre * sig * up_pre).astype(BF16)
    summed = lax.psum_scatter(
        dot_nn(hidden, w_d).astype(BF16), "dp", scatter_dimension=1, tiled=True
    )
    returned = exchange(summed, experts).astype(F32)
    mixed = spread_rows(picker_tb, returned * slot_gate[:, None]).astype(BF16)
    dy_rows = dot_nn(pick_b, grad_out)
    score = lax.psum(jnp.sum(dy_rows * returned, axis=1), "dp")
    dy_own = exchange((dy_rows * slot_gate[:, None]).astype(BF16), experts)
    dy_slots = lax.all_gather(dy_own, "dp", axis=1, tiled=True)
    d_hidden = dot_nt(dy_slots, w_d)
    d_gate = (d_hidden * up_pre * sig * (1.0 + gate_pre * (1.0 - sig))).astype(BF16)
    d_up = (d_hidden * gate_pre * sig).astype(BF16)
    grad_down = dot_tn(hidden, dy_slots).astype(BF16)
    grad_gate = dot_tn(rows, d_gate).astype(BF16)
    grad_up = dot_tn(rows, d_up).astype(BF16)
    input_rows = dot_nt(d_gate, w_g) + dot_nt(d_up, w_u)
    input_summed = lax.psum_scatter(
        input_rows.astype(BF16), "dp", scatter_dimension=1, tiled=True
    )
    grad_tokens = dot_nn(picker_tb, exchange(input_summed, experts)).astype(BF16)
    grad_gates = jnp.dot(score, match, precision=lax.Precision.HIGHEST).reshape(tok, top)
    return mixed, grad_tokens, grad_gates, grad_gate[None], grad_up[None], grad_down[None]


def in_pairs(mesh, width, hid):
    return mesh.shape["dp"] == 2 and width % (2 * STEP) == 0 and hid % (2 * STEP) == 0


def solution(mesh):
    placed = (
        P("expert", None),
        P("expert", None),
        P("expert", None),
        P("expert"),
        P("expert", None, "dp"),
        P("expert", None, "dp"),
        P("expert", "dp", None),
        P("expert", "dp"),
    )
    over = functools.partial(
        jax.shard_map,
        mesh=mesh,
        in_specs=placed,
        out_specs=(
            P("expert", "dp"),
            P("expert", "dp"),
            P("expert", None),
            P("expert", None, "dp"),
            P("expert", None, "dp"),
            P("expert", "dp", None),
        ),
        check_vma=False,
    )

    def layer(*args):
        if not in_pairs(mesh, *args[4].shape[1:]):
            return over(shared)(*args)
        return over(paired)(*args)

    return layer
```

time: 201 us -> 145 us (0.72)
  waiting for transfers between devices: 79.2 us -> 32.7 us
  matrix products: 63.7 us -> 18.7 us
  Pallas kernels: 0 us -> 40 us
  local copies, waits for them, and re-layouts: 4.05 us -> 19.9 us
  between operations: 14.8 us -> 1.62 us
  other arithmetic: 6.98 us -> 4.13 us
  blocking collectives: 2.69 us -> 0 us
    dot_general x17 -> x3, matrix products: 63.7 us -> 18.7 us  [dot_tn(): lax.dot_general(a, b, (((0,), (0,)), ((), ())), preferred_element_type=F32)]
    all_to_all x4, waiting for transfers between devices: 73.6 us -> 32.6 us  [exchange(): lax.all_to_all(x.reshape(experts, rows // experts, width), 'expert', 0, 0...]
    pallas_call x0 -> x14, Pallas kernels: none -> 40 us  [the longest x13 36.7 us: call(): pl.pallas_call(kernel, in_specs=specs or [SMEM] + [VMEM] * (len(args) - 1...]
    unnamed x37 -> x44, local copies, waits for them, and re-layouts: 2.62 us -> 19.9 us
    reduce_scatter x2 -> x0, waiting for transfers between devices: 4.91 us -> none  [the longest x1 4.54 us: on_device(): lax.psum_scatter(input_rows.reshape(experts, SLOTS, width).astype(jnp.bfl...]
    another operation x2 -> x0, other arithmetic: 4.71 us -> none
    convert_element_type x1 -> x2, other arithmetic: 0.02 us -> 3.46 us  [the longest x1 2.3 us: paired(): y_sum = (y_near + y_far.astype(F32)).astype(BF16)]
    psum x1 -> x0, blocking collectives: 2.69 us -> none  [on_device(): score = lax.psum(jnp.sum(dy_rows * returned, axis=1), 'dp')]
  transfers between devices with their start and end apart: 7 -> 9, of which waited for: 5 -> 4; matrix products, arithmetic and copies ran while one was open for 20% -> 16% of each run, Pallas kernels for 0% -> 25%
where the time goes in v1:
time: 145 us; the launch traced here: 144 us
  Pallas kernels  40 us (28%)
  waiting for transfers between devices  32.7 us (23%)
  starting transfers between devices  26.8 us (18%)
  local copies, waits for them, and re-layouts  19.9 us (14%)
  matrix products  18.7 us (13%)
  other arithmetic  4.13 us (3%)
  between operations  1.62 us (1%)
    pallas_call x13, Pallas kernels, call(): pl.pallas_call(kernel, in_specs=specs or [SMEM] + [VMEM] * (len(args) - 1...  36.7 us
    all_to_all x4, waiting for transfers between devices, exchange(): lax.all_to_all(x.reshape(experts, rows // experts, width), 'expert', 0, 0...  32.6 us
    all_to_all x4, starting transfers between devices, exchange(): lax.all_to_all(x.reshape(experts, rows // experts, width), 'expert', 0, 0...  26.3 us
    unnamed x44, local copies, waits for them, and re-layouts  19.9 us
    dot_general x3, matrix products, dot_tn(): lax.dot_general(a, b, (((0,), (0,)), ((), ())), preferred_element_type=F32)  18.7 us
    pallas_call x1, Pallas kernels, paired(): pl.pallas_call(dispatch_kernel, grid_spec=pltpu.PrefetchScalarGridSpec(nu...  3.35 us
  transfers between devices with their start and end apart: 9, of which 4 were waited for; matrix products, arithmetic and copies ran while one was open for 16% of the time, Pallas kernels for 25%

profile of v1, /device:TPU:0, one launch (start us, length us, event | category | flops | bytes accessed | tf_op | source)
XLA Modules:
  0.0 143.9 jit_solution(5618119838171282884)
XLA Ops:
  0.6 0.0 copy-start.11
  1.4 0.1 pad_add_fusion.where_ref
  1.4 3.4 %dispatch.1 = (bf16[256,1792]{1,0:T(8,128)(2,1)}, bf16[256,256]{1,0:T(8,128)(2,1)S(1)}, f32[256,256]{1,0:T(8,128)S(1)}) custom-call(s32[2]{0:T(128)S(1)} %pad_add_fusion.where_ref, s32[8,256]{1,0:T(8,128)} %bitcast.33, f32[8,256]{1,0:T(8,128)} %bitcast.43, bf16[256,3584]{1,0:T(8,128)(2,1)} %tok_ref.1), custom_call_target="tpu_custom_call" | custom-call | tf_op jit(solution)/shard_map/dispatch/pallas_call | solution.py:240
  4.8 8.3 %all-to-all-start = ((bf16[16,16,1792]{2,1,0:T(8,128)(2,1)}), bf16[16,16,1792]{2,1,0:T(8,128)(2,1)S(1)}, u32[]{:S(2)}, u32[]{:S(2)}) async-start(bf16[16,16,1792]{2,1,0:T(8,128)(2,1)} %bitcast.3), calls=%async_computation | async-start | bytes 1835008 | tf_op jit(solution)/shard_map/all_to_all | solution.py:220
  13.2 1.3 shard_map.127
  14.5 20.6 %all-to-all-done = bf16[16,16,1792]{2,1,0:T(8,128)(2,1)S(1)} async-done(((bf16[16,16,1792]{2,1,0:T(8,128)(2,1)}), bf16[16,16,1792]{2,1,0:T(8,128)(2,1)S(1)}, u32[]{:S(2)}, u32[]{:S(2)}) %all-to-all-start) | async-done | bytes 917536 | tf_op jit(solution)/shard_map/all_to_all | solution.py:220
  35.1 5.5 %all-to-all-start.2 = ((bf16[16,16,1792]{2,1,0:T(8,128)(2,1)}), bf16[16,16,1792]{2,1,0:T(8,128)(2,1)S(1)}, u32[]{:S(2)}, u32[]{:S(2)}) async-start(bf16[16,16,1792]{2,1,0:T(8,128)(2,1)} %bitcast.10), calls=%async_computation.2 | async-start | bytes 1835008 | tf_op jit(solution)/shard_map/all_to_all | solution.py:220
  40.6 5.3 %shard_map.128 = (bf16[3584,1024]{1,0:T(8,128)(2,1)S(1)}, bf16[3584,1024]{1,0:T(8,128)(2,1)S(1)}) custom-call(bf16[3584,1024]{1,0:T(8,128)(2,1)} %bitcast.37, bf16[3584,1024]{1,0:T(8,128)(2,1)} %bitcast.39), custom_call_target="tpu_custom_call" | custom-call | bytes 29360128 | tf_op jit(solution)/shard_map/pallas_call | solution.py:194
  46.0 4.5 %shard_map.129 = (f32[256,1024]{1,0:T(8,128)S(1)}, f32[256,1024]{1,0:T(8,128)S(1)}, bf16[1024,3584]{1,0:T(8,128)(2,1)S(1)}) custom-call(s32[1]{0:T(128)} %bitcast.part_ref, bf16[256,1792]{1,0:T(8,128)(2,1)S(1)} %bitcast.27, bf16[3584,1024]{1,0:T(8,128)(2,1)S(1)} %get-tuple-element.30.wg_ref, bf16[3584,1024]{1,0:T(8,128)(2,1)S(1)} %get-tuple-element.31.wu_ref, ...), custom_call_target="tpu_custom_call" | custom-call | flops 1879048192 | bytes 32374788 | tf_op jit(solution)/shard_map/pallas_call | solution.py:194
  50.5 0.0 copy-start.6
  50.5 2.3 %shard_map.130 = (bf16[256,1024]{1,0:T(8,128)(2,1)S(1)}, bf16[256,1024]{1,0:T(8,128)(2,1)S(1)}, bf16[256,1024]{1,0:T(8,128)(2,1)S(1)}) custom-call(s32[1]{0:T(128)S(6)} %sub.3.part_ref, bf16[256,1792]{1,0:T(8,128)(2,1)S(1)} %collective-permute-done.x_ref, bf16[3584,1024]{1,0:T(8,128)(2,1)S(1)} %get-tuple-element.30.wg_ref, ...), custom_call_target="tpu_custom_call" | custom-call | flops 1879048192 | bytes 19267588 | tf_op jit(solution)/shard_map/pallas_call | solution.py:194
  52.8 0.2 copy-done.13
  53.0 0.8 copy-done.6
  53.8 2.1 %shard_map.132 = bf16[256,1792]{1,0:T(8,128)(2,1)} custom-call(s32[1]{0:T(128)S(6)} %sub.3.part_ref, bf16[256,1024]{1,0:T(8,128)(2,1)S(1)} %get-tuple-element.34.h_ref, bf16[1024,3584]{1,0:T(8,128)(2,1)S(1)} %get-tuple-element.35.w_ref), custom_call_target="tpu_custom_call" | custom-call | flops 939524096 | bytes 8781828 | tf_op jit(solution)/shard_map/pallas_call | solution.py:194
  55.9 0.2 collective-permute-start.1
  56.1 6.9 %all-to-all-done.2 = bf16[16,16,1792]{2,1,0:T(8,128)(2,1)S(1)} async-done(((bf16[16,16,1792]{2,1,0:T(8,128)(2,1)}), bf16[16,16,1792]{2,1,0:T(8,128)(2,1)S(1)}, u32[]{:S(2)}, u32[]{:S(2)}) %all-to-all-start.2) | async-done | bytes 917536 | tf_op jit(solution)/shard_map/all_to_all | solution.py:220
  63.0 3.3 %shard_map.134.w_ref = bf16[1024,3584]{1,0:T(8,128)(2,1)S(1)} custom-call(bf16[1024,3584]{1,0:T(8,128)(2,1)} %bitcast.36), custom_call_target="tpu_custom_call" | custom-call | bytes 14680064 | tf_op jit(solution)/shard_map/pallas_call | solution.py:194
  66.3 1.9 %copy-done.7 = bf16[1024,3584]{1,0:T(8,128)(2,1)S(1)} copy-done((bf16[1024,3584]{1,0:T(8,128)(2,1)S(1)}, bf16[1024,3584]{1,0:T(8,128)(2,1)}, u32[]{:S(2)}) %copy-start.7) | copy-done | bytes 7340056
  68.3 1.1 shard_map.131
  69.4 1.9 %copy-done = bf16[1024,3584]{1,0:T(8,128)(2,1)} copy-done((bf16[1024,3584]{1,0:T(8,128)(2,1)}, bf16[1024,3584]{1,0:T(8,128)(2,1)S(1)}, u32[]{:S(2)}) %copy-start) | copy-done | bytes 7340056
  71.3 5.3 %shard_map.135 = (f32[256,1024]{1,0:T(8,128)S(1)}, bf16[3584,1024]{1,0:T(8,128)(2,1)S(1)}, bf16[3584,1024]{1,0:T(8,128)(2,1)S(1)}) custom-call(s32[1]{0:T(128)} %bitcast.part_ref, bf16[256,1792]{1,0:T(8,128)(2,1)S(1)} %bitcast.31, bf16[1024,3584]{1,0:T(8,128)(2,1)S(1)} %shard_map.134.w_ref, bf16[3584,1024]{1,0:T(8,128)(2,1)} %bitcast.38, ...), custom_call_target="tpu_custom_call" | custom-call | flops 939524096 | bytes 38666244 | tf_op jit(solution)/shard_map/pallas_call | solution.py:194
  76.6 0.0 copy-start.2
  76.6 3.0 %copy-done.2 = bf16[3584,1024]{1,0:T(8,128)(2,1)} copy-done((bf16[3584,1024]{1,0:T(8,128)(2,1)}, bf16[3584,1024]{1,0:T(8,128)(2,1)S(1)}, u32[]{:S(2)}) %copy-start.2) | copy-done | bytes 7340056
  79.7 3.0 %copy-done.4 = bf16[3584,1024]{1,0:T(8,128)(2,1)} copy-done((bf16[3584,1024]{1,0:T(8,128)(2,1)}, bf16[3584,1024]{1,0:T(8,128)(2,1)S(1)}, u32[]{:S(2)}) %copy-start.4) | copy-done | bytes 7340056
  82.7 2.3 %add_convert_fusion.1 = bf16[256,1792]{1,0:T(8,128)(2,1)} fusion(f32[256,1792]{1,0:T(8,128)S(1)} %shard_map.131, bf16[256,1792]{1,0:T(8,128)(2,1)} %collective-permute-done.1), kind=kLoop, calls=%fused_computation.14 | loop fusion | flops 1376256 | bytes 3670016 | tf_op jit(solution)/shard_map/convert_element_type | solution.py:286
  85.0 6.2 %all-to-all-start.1 = ((bf16[16,16,1792]{2,1,0:T(8,128)(2,1)}), bf16[16,16,1792]{2,1,0:T(8,128)(2,1)}, u32[]{:S(2)}, u32[]{:S(2)}) async-start(bf16[16,16,1792]{2,1,0:T(8,128)(2,1)} %bitcast.42), calls=%async_computation.1 | async-start | bytes 1835008 | tf_op jit(solution)/shard_map/all_to_all | solution.py:220
  91.3 0.0 copy-start.1
  91.3 3.1 %copy-done.1 = bf16[1024,3584]{1,0:T(8,128)(2,1)S(1)} copy-done((bf16[1024,3584]{1,0:T(8,128)(2,1)S(1)}, bf16[1024,3584]{1,0:T(8,128)(2,1)}, u32[]{:S(2)}) %copy-start.1) | copy-done | bytes 7340056
  94.4 1.0 copy-done.16
  95.4 1.0 copy-done.18
  96.5 2.6 %shard_map.136 = (bf16[256,1024]{1,0:T(8,128)(2,1)S(1)}, bf16[256,1024]{1,0:T(8,128)(2,1)S(1)}) custom-call(s32[1]{0:T(128)S(6)} %sub.3.part_ref, bf16[256,1792]{1,0:T(8,128)(2,1)} %collective-permute-done.2.dy_ref, bf16[1024,3584]{1,0:T(8,128)(2,1)S(1)} %copy-done.1, f32[256,1024]{1,0:T(8,128)S(1)} %get-tuple-element.38.dh0_ref, ...), custom_call_target="tpu_custom_call" | custom-call | flops 939524096 | bytes 11403268 | tf_op jit(solution)/shard_map/pallas_call | solution.py:194
  99.1 0.0 copy-start.10
  99.1 0.8 copy-done.3
  99.8 3.1 %copy-done.5 = bf16[3584,1024]{1,0:T(8,128)(2,1)S(1)} copy-done((bf16[3584,1024]{1,0:T(8,128)(2,1)S(1)}, bf16[3584,1024]{1,0:T(8,128)(2,1)}, u32[]{:S(2)}) %copy-start.5) | copy-done | bytes 7340056
  102.9 2.1 %shard_map.138 = bf16[256,1792]{1,0:T(8,128)(2,1)S(1)} custom-call(s32[1]{0:T(128)S(6)} %sub.3.part_ref, bf16[256,1024]{1,0:T(8,128)(2,1)S(1)} %get-tuple-element.41.dg_ref, bf16[256,1024]{1,0:T(8,128)(2,1)S(1)} %get-tuple-element.42.du_ref, bf16[3584,1024]{1,0:T(8,128)(2,1)S(1)} %copy-done.3, bf16[3584,1024]{1,0:T(8,128)(2,1)S(1)} %copy-done.5), custom_call_target="tpu_custom_call" | custom-call | flops 1879048192 | bytes 16646148 | tf_op jit(solution)/shard_map/pallas_call | solution.py:194
  105.0 0.3 collective-permute-start.3
  105.3 2.1 %shard_map.137 = f32[256,1792]{1,0:T(8,128)S(1)} custom-call(s32[1]{0:T(128)} %bitcast.part_ref, bf16[256,1024]{1,0:T(8,128)(2,1)S(1)} %get-tuple-element.41.dg_ref, bf16[256,1024]{1,0:T(8,128)(2,1)S(1)} %get-tuple-element.42.du_ref, bf16[3584,1024]{1,0:T(8,128)(2,1)S(1)} %copy-done.3, bf16[3584,1024]{1,0:T(8,128)(2,1)S(1)} %copy-done.5), custom_call_target="tpu_custom_call" | custom-call | flops 1879048192 | bytes 17563652 | tf_op jit(solution)/shard_map/pallas_call | solution.py:194
  107.4 0.1 collective-permute-done.3
  107.5 1.2 add_convert_fusion
  108.7 5.0 %all-to-all-done.1 = bf16[16,16,1792]{2,1,0:T(8,128)(2,1)} async-done(((bf16[16,16,1792]{2,1,0:T(8,128)(2,1)}), bf16[16,16,1792]{2,1,0:T(8,128)(2,1)}, u32[]{:S(2)}, u32[]{:S(2)}) %all-to-all-start.1) | async-done | bytes 917536 | tf_op jit(solution)/shard_map/all_to_all | solution.py:220
  113.7 6.2 %all-to-all-start.3 = ((bf16[16,16,1792]{2,1,0:T(8,128)(2,1)}), bf16[16,16,1792]{2,1,0:T(8,128)(2,1)S(1)}, u32[]{:S(2)}, u32[]{:S(2)}) async-start(bf16[16,16,1792]{2,1,0:T(8,128)(2,1)} %bitcast.41), calls=%async_computation.3 | async-start | bytes 1835008 | tf_op jit(solution)/shard_map/all_to_all | solution.py:220
  119.9 0.0 copy-start.9
  120.0 6.9 %fusion = bf16[1,3584,1024]{2,1,0:T(8,128)(2,1)} fusion(bf16[256,1024]{1,0:T(8,128)(2,1)} %copy-done.10, bf16[256,1792]{1,0:T(8,128)(2,1)} %copy-done.13, bf16[256,1792]{1,0:T(8,128)(2,1)S(1)} %bitcast.28, pred[]{:T(512)S(6)} %eq.3), kind=kOutput, calls=%fused_computation.3 | convolution fusion | flops 1890975744 | bytes 9699329 | tf_op jit(solution)/shard_map/dot_general | solution.py:41
  126.9 5.2 %fusion.1 = bf16[1,3584,1024]{2,1,0:T(8,128)(2,1)} fusion(bf16[256,1024]{1,0:T(8,128)(2,1)S(1)} %copy-done.9, bf16[256,1792]{1,0:T(8,128)(2,1)S(1)} %copy-done.14, bf16[256,1792]{1,0:T(8,128)(2,1)S(1)} %bitcast.29, pred[]{:T(512)S(6)} %eq.3), kind=kOutput, calls=%fused_computation.4 | convolution fusion | flops 1890975744 | bytes 9699329 | tf_op jit(solution)/shard_map/dot_general | solution.py:41
  132.1 3.2 %shard_map.133 = (bf16[256,1792]{1,0:T(8,128)(2,1)}, f32[8,256]{1,0:T(8,128)S(1)}) custom-call(bf16[256,256]{1,0:T(8,128)(2,1)S(1)} %get-tuple-element.26.pick_ref, f32[256,256]{1,0:T(8,128)S(1)} %copy-done.20, s32[8,256]{1,0:T(8,128)S(1)} %bitcast.34, bf16[256,1792]{1,0:T(8,128)(2,1)} %bitcast.9.back_ref, bf16[256,1792]{1,0:T(8,128)(2,1)S(1)} %copy-done.12), custom_call_target="tpu_custom_call" | custom-call | flops 704643072 | bytes 3162112 | tf_op jit(solution)/shard_map/pallas_call | solution.py:194
  135.3 6.6 %fusion.2 = bf16[1,1024,3584]{2,1,0:T(8,128)(2,1)} fusion(bf16[256,1024]{1,0:T(8,128)(2,1)S(1)} %get-tuple-element.34.h_ref, bf16[256,1792]{1,0:T(8,128)(2,1)} %collective-permute-done.2.dy_ref, bf16[256,1792]{1,0:T(8,128)(2,1)S(1)} %bitcast.32, pred[]{:T(512)S(6)} %eq.3), kind=kOutput, calls=%fused_computation.5 | convolution fusion | flops 1890975744 | bytes 9699329 | tf_op jit(solution)/shard_map/dot_general | solution.py:41
  141.9 0.6 add_bitcast_fusion
  142.5 1.4 shard_map.139
  (35 shorter events, 0.1 us)
Async XLA Ops:
  0.6 12.5 %copy-start.11 = (bf16[256,1792]{1,0:T(8,128)(2,1)S(1)}, bf16[256,1792]{1,0:T(8,128)(2,1)}, u32[]{:S(2)}) copy-start(bf16[256,1792]{1,0:T(8,128)(2,1)} %out_ref.3) | copy-start | bytes 2752516
  4.8 41.1 %copy-start.19 = (f32[256,256]{1,0:T(8,128)}, f32[256,256]{1,0:T(8,128)S(1)}, u32[]{:S(2)}) copy-start(f32[256,256]{1,0:T(8,128)S(1)} %get-tuple-element.27.weight_ref) | copy-start | bytes 786436
  4.8 30.3 %all-to-all-start = ((bf16[16,16,1792]{2,1,0:T(8,128)(2,1)}), bf16[16,16,1792]{2,1,0:T(8,128)(2,1)S(1)}, u32[]{:S(2)}, u32[]{:S(2)}) async-start(bf16[16,16,1792]{2,1,0:T(8,128)(2,1)} %bitcast.3), calls=%async_computation | async-start | bytes 1835008 | tf_op jit(solution)/shard_map/all_to_all | solution.py:220
  35.1 15.3 %collective-permute-start = (bf16[256,1792]{1,0:T(8,128)(2,1)S(1)}, bf16[256,1792]{1,0:T(8,128)(2,1)S(1)}, u32[]{:S(2)}, u32[]{:S(2)}) collective-permute-start(bf16[256,1792]{1,0:T(8,128)(2,1)S(1)} %bitcast.26), channel_id=1, source_target_pairs={{0,1},{1,0},{2,3},{3,2},{4,5},{5,4},{6,7},{7,6},{8,9},{9,8},{10,11... | collective-permute-start | bytes 2752520 | tf_op jit(solution)/shard_map/ppermute | solution.py:215
  35.1 27.9 %all-to-all-start.2 = ((bf16[16,16,1792]{2,1,0:T(8,128)(2,1)}), bf16[16,16,1792]{2,1,0:T(8,128)(2,1)S(1)}, u32[]{:S(2)}, u32[]{:S(2)}) async-start(bf16[16,16,1792]{2,1,0:T(8,128)(2,1)} %bitcast.10), calls=%async_computation.2 | async-start | bytes 1835008 | tf_op jit(solution)/shard_map/all_to_all | solution.py:220
  50.5 3.3 %copy-start.6 = (bf16[1024,3584]{1,0:T(8,128)(2,1)}, bf16[1024,3584]{1,0:T(8,128)(2,1)S(1)}, u32[]{:S(2)}) copy-start(bf16[1024,3584]{1,0:T(8,128)(2,1)S(1)} %get-tuple-element.35.w_ref) | copy-start | bytes 22020100
  50.5 2.5 %copy-start.13 = (bf16[256,1792]{1,0:T(8,128)(2,1)}, bf16[256,1792]{1,0:T(8,128)(2,1)S(1)}, u32[]{:S(2)}) copy-start(bf16[256,1792]{1,0:T(8,128)(2,1)S(1)} %collective-permute-done.x_ref) | copy-start | bytes 2752516
  53.0 2.9 %copy-start.15 = (bf16[256,1024]{1,0:T(8,128)(2,1)}, bf16[256,1024]{1,0:T(8,128)(2,1)S(1)}, u32[]{:S(2)}) copy-start(bf16[256,1024]{1,0:T(8,128)(2,1)S(1)} %get-tuple-element.39.a_ref) | copy-start | bytes 1572868
  53.0 2.9 %copy-start.17 = (bf16[256,1024]{1,0:T(8,128)(2,1)}, bf16[256,1024]{1,0:T(8,128)(2,1)S(1)}, u32[]{:S(2)}) copy-start(bf16[256,1024]{1,0:T(8,128)(2,1)S(1)} %get-tuple-element.40.b_ref) | copy-start | bytes 1572868
  55.9 26.9 %collective-permute-start.1 = (bf16[256,1792]{1,0:T(8,128)(2,1)}, bf16[256,1792]{1,0:T(8,128)(2,1)}, u32[]{:S(2)}, u32[]{:S(2)}) collective-permute-start(bf16[256,1792]{1,0:T(8,128)(2,1)} %shard_map.132), channel_id=1, source_target_pairs={{0,1},{1,0},{2,3},{3,2},{4,5},{5,4},{6,7},{7,6},{8,9},{9,8},{10,11... | collective-permute-start | bytes 2752520 | tf_op jit(solution)/shard_map/ppermute | solution.py:215
  63.0 28.3 %collective-permute-start.2 = (bf16[256,1792]{1,0:T(8,128)(2,1)S(1)}, bf16[256,1792]{1,0:T(8,128)(2,1)}, u32[]{:S(2)}, u32[]{:S(2)}) collective-permute-start(bf16[256,1792]{1,0:T(8,128)(2,1)S(1)} %bitcast.30), channel_id=1, source_target_pairs={{0,1},{1,0},{2,3},{3,2},{4,5},{5,4},{6,7},{7,6},{8,9},{9,8},{10,11... | collective-permute-start | bytes 2752520 | tf_op jit(solution)/shard_map/ppermute | solution.py:215
  63.0 5.2 %copy-start.7 = (bf16[1024,3584]{1,0:T(8,128)(2,1)S(1)}, bf16[1024,3584]{1,0:T(8,128)(2,1)}, u32[]{:S(2)}) copy-start(bf16[1024,3584]{1,0:T(8,128)(2,1)} %copy-done.6) | copy-start | bytes 22020100
  68.3 3.0 %copy-start = (bf16[1024,3584]{1,0:T(8,128)(2,1)}, bf16[1024,3584]{1,0:T(8,128)(2,1)S(1)}, u32[]{:S(2)}) copy-start(bf16[1024,3584]{1,0:T(8,128)(2,1)S(1)} %shard_map.134.w_ref) | copy-start | bytes 22020100
  76.6 3.1 %copy-start.2 = (bf16[3584,1024]{1,0:T(8,128)(2,1)}, bf16[3584,1024]{1,0:T(8,128)(2,1)S(1)}, u32[]{:S(2)}) copy-start(bf16[3584,1024]{1,0:T(8,128)(2,1)S(1)} %get-tuple-element.43.wg_ref) | copy-start | bytes 22020100
  79.7 3.0 %copy-start.4 = (bf16[3584,1024]{1,0:T(8,128)(2,1)}, bf16[3584,1024]{1,0:T(8,128)(2,1)S(1)}, u32[]{:S(2)}) copy-start(bf16[3584,1024]{1,0:T(8,128)(2,1)S(1)} %get-tuple-element.44.wu_ref) | copy-start | bytes 22020100
  85.0 28.7 %all-to-all-start.1 = ((bf16[16,16,1792]{2,1,0:T(8,128)(2,1)}), bf16[16,16,1792]{2,1,0:T(8,128)(2,1)}, u32[]{:S(2)}, u32[]{:S(2)}) async-start(bf16[16,16,1792]{2,1,0:T(8,128)(2,1)} %bitcast.42), calls=%async_computation.1 | async-start | bytes 1835008 | tf_op jit(solution)/shard_map/all_to_all | solution.py:220
  91.3 3.1 %copy-start.1 = (bf16[1024,3584]{1,0:T(8,128)(2,1)S(1)}, bf16[1024,3584]{1,0:T(8,128)(2,1)}, u32[]{:S(2)}) copy-start(bf16[1024,3584]{1,0:T(8,128)(2,1)} %copy-done) | copy-start | bytes 22020100
  94.4 1.0 copy-start.16
  95.4 1.0 copy-start.18
  96.5 3.4 %copy-start.3 = (bf16[3584,1024]{1,0:T(8,128)(2,1)S(1)}, bf16[3584,1024]{1,0:T(8,128)(2,1)}, u32[]{:S(2)}) copy-start(bf16[3584,1024]{1,0:T(8,128)(2,1)} %copy-done.2) | copy-start | bytes 22020100
  99.0 6.3 %copy-start.8 = (bf16[256,1024]{1,0:T(8,128)(2,1)}, bf16[256,1024]{1,0:T(8,128)(2,1)S(1)}, u32[]{:S(2)}) copy-start(bf16[256,1024]{1,0:T(8,128)(2,1)S(1)} %get-tuple-element.42.du_ref) | copy-start | bytes 1572868
  99.1 6.2 %copy-start.10 = (bf16[256,1024]{1,0:T(8,128)(2,1)}, bf16[256,1024]{1,0:T(8,128)(2,1)S(1)}, u32[]{:S(2)}) copy-start(bf16[256,1024]{1,0:T(8,128)(2,1)S(1)} %get-tuple-element.41.dg_ref) | copy-start | bytes 1572868
  99.8 3.1 %copy-start.5 = (bf16[3584,1024]{1,0:T(8,128)(2,1)S(1)}, bf16[3584,1024]{1,0:T(8,128)(2,1)}, u32[]{:S(2)}) copy-start(bf16[3584,1024]{1,0:T(8,128)(2,1)} %copy-done.4) | copy-start | bytes 22020100
  105.0 2.5 %collective-permute-start.3 = (bf16[256,1792]{1,0:T(8,128)(2,1)S(1)}, bf16[256,1792]{1,0:T(8,128)(2,1)S(1)}, u32[]{:S(2)}, u32[]{:S(2)}) collective-permute-start(bf16[256,1792]{1,0:T(8,128)(2,1)S(1)} %shard_map.138), channel_id=1, source_target_pairs={{0,1},{1,0},{2,3},{3,2},{4,5},{5,4},{6,7},{7,6},{8,9},{9,8},{10,11... | collective-permute-start | bytes 2752520 | tf_op jit(solution)/shard_map/ppermute | solution.py:215
  113.7 28.8 %all-to-all-start.3 = ((bf16[16,16,1792]{2,1,0:T(8,128)(2,1)}), bf16[16,16,1792]{2,1,0:T(8,128)(2,1)S(1)}, u32[]{:S(2)}, u32[]{:S(2)}) async-start(bf16[16,16,1792]{2,1,0:T(8,128)(2,1)} %bitcast.41), calls=%async_computation.3 | async-start | bytes 1835008 | tf_op jit(solution)/shard_map/all_to_all | solution.py:220
  119.9 6.9 %copy-start.9 = (bf16[256,1024]{1,0:T(8,128)(2,1)S(1)}, bf16[256,1024]{1,0:T(8,128)(2,1)}, u32[]{:S(2)}) copy-start(bf16[256,1024]{1,0:T(8,128)(2,1)} %copy-done.8) | copy-start | bytes 1572868
  119.9 6.9 %copy-start.14 = (bf16[256,1792]{1,0:T(8,128)(2,1)S(1)}, bf16[256,1792]{1,0:T(8,128)(2,1)}, u32[]{:S(2)}) copy-start(bf16[256,1792]{1,0:T(8,128)(2,1)} %copy-done.13) | copy-start | bytes 2752516
  126.9 5.2 %copy-start.12 = (bf16[256,1792]{1,0:T(8,128)(2,1)S(1)}, bf16[256,1792]{1,0:T(8,128)(2,1)}, u32[]{:S(2)}) copy-start(bf16[256,1792]{1,0:T(8,128)(2,1)} %out_ref.3) | copy-start | bytes 2752516
  126.9 5.2 %copy-start.20 = (f32[256,256]{1,0:T(8,128)S(1)}, f32[256,256]{1,0:T(8,128)}, u32[]{:S(2)}) copy-start(f32[256,256]{1,0:T(8,128)} %copy-done.19) | copy-start | bytes 786436
  126.9 5.2 %copy-start.21 = (s32[256,8]{0,1:T(8,128)S(1)}, s32[256,8]{0,1:T(8,128)}, u32[]{:S(2)}) copy-start(s32[256,8]{0,1:T(8,128)} %param.9) | copy-start | bytes 24580
  135.3 6.6 %collective-permute-start.4 = (f32[8,256]{1,0:T(8,128)S(1)}, f32[8,256]{1,0:T(8,128)S(1)}, u32[]{:S(2)}, u32[]{:S(2)}) collective-permute-start(f32[8,256]{1,0:T(8,128)S(1)} %get-tuple-element.45), channel_id=1, source_target_pairs={{0,1},{1,0},{2,3},{3,2},{4,5},{5,4},{6,7},{7,6},{8,9},{9,8},{10,11... | collective-permute-start | bytes 24584 | tf_op jit(solution)/shard_map/ppermute | solution.py:215

commit v2 on v1

--- a/solution.py
+++ b/solution.py
@@ -18,6 +18,7 @@
 SMEM = pl.BlockSpec(memory_space=pltpu.SMEM)
 STEP = 256
 PARTS = 4
+PIECES = 2
 DMAS = pltpu.SemaphoreType.DMA((PARTS,))
 
 
@@ -41,29 +42,64 @@
     return lax.dot_general(a, b, (((0,), (0,)), ((), ())), preferred_element_type=F32)
 
 
-def dispatch_kernel(where_ref, ids_ref, gates_ref, tok_ref, send_ref, pick_ref, weight_ref):
-    top, tok = ids_ref.shape
-    queue = pick_ref.shape[0]
+def pieces(src, dst, sems, src_first=0, dst_first=0):
+    wide = min(src.shape[1], dst.shape[1]) // PIECES
+    return [
+        pltpu.make_async_copy(
+            src.at[:, pl.ds(pl.multiple_of(src_first + i * wide, 128), wide)],
+            dst.at[:, pl.ds(pl.multiple_of(dst_first + i * wide, 128), wide)],
+            sems.at[i],
+        )
+        for i in range(PIECES)
+    ]
+
+
+def dispatch_kernel(
+    part_ref, tiles_ref, ids_ref, gates_ref, tok_ref, send_ref, pick_ref, weight_ref,
+    ids_v, gates_v, tok_v, send_v, pick_v, weight_v, near_s, in_s, out_s,
+):
+    top, tok = ids_v.shape
+    queue, half = send_v.shape
+    named_in = [
+        pltpu.make_async_copy(ids_ref, ids_v, near_s.at[0]),
+        pltpu.make_async_copy(gates_ref, gates_v, near_s.at[1]),
+    ]
+    tables = [
+        pltpu.make_async_copy(pick_v, pick_ref, near_s.at[2]),
+        pltpu.make_async_copy(weight_v, weight_ref, near_s.at[3]),
+    ]
+    ins = pieces(tok_ref, tok_v, in_s, part_ref[0] * half)
+    outs = pieces(send_v, send_ref, out_s)
+    begin(named_in + ins)
     owner = lax.broadcasted_iota(jnp.int32, (queue, tok), 0)
     expert, slot = owner // SLOTS, owner % SLOTS
-    ids, gates = ids_ref[...], gates_ref[...]
+    before = lax.broadcasted_iota(jnp.int32, (tok, tok), 0) < lax.broadcasted_iota(
+        jnp.int32, (tok, tok), 1
+    )
+    earlier = jnp.where(before, 1.0, 0.0).astype(BF16)
+    live = lax.broadcasted_iota(jnp.int32, (1, tok), 1) < tiles_ref[0] * TILE
+    finish(named_in)
+    ids = jnp.where(live, ids_v[...], -1)
+    gates = gates_v[...]
     named = jnp.zeros((queue, tok), F32)
     weight = jnp.zeros((queue, tok), F32)
     for k in range(top):
         hit = jnp.broadcast_to(ids[k : k + 1, :], (queue, tok)) == expert
         named = jnp.where(hit, 1.0, named)
         weight = jnp.where(hit, jnp.broadcast_to(gates[k : k + 1, :], (queue, tok)), weight)
-    live = lax.broadcasted_iota(jnp.int32, (queue, tok), 1) < where_ref[1] * TILE
-    named = jnp.where(live, named, 0.0)
-    before = lax.broadcasted_iota(jnp.int32, (tok, tok), 0) < lax.broadcasted_iota(
-        jnp.int32, (tok, tok), 1
-    )
-    rank = dot_nn(named.astype(BF16), jnp.where(before, 1.0, 0.0).astype(BF16))
+    rank = dot_nn(named.astype(BF16), earlier)
     chosen = (named > 0.5) & (rank == slot.astype(F32))
     pick = jnp.where(chosen, 1.0, 0.0).astype(BF16)
-    send_ref[...] = dot_nn(pick, tok_ref[...]).astype(BF16)
-    pick_ref[...] = pick
-    weight_ref[...] = jnp.where(chosen, weight, 0.0)
+    pick_v[...] = pick
+    weight_v[...] = jnp.where(chosen, weight, 0.0)
+    begin(tables)
+    wide = half // PIECES
+    for i in range(PIECES):
+        c = slice(i * wide, (i + 1) * wide)
+        ins[i].wait()
+        send_v[:, c] = dot_nn(pick, tok_v[:, c]).astype(BF16)
+        outs[i].start()
+    finish(outs + tables)
 
 
 def cotangent_kernel(pick_ref, weight_ref, out_ref, send_ref):
@@ -71,13 +107,23 @@
     send_ref[...] = (dot_nn(pick_ref[...], out_ref[...]) * gate).astype(BF16)
 
 
-def combine_kernel(pick_ref, weight_ref, ids_ref, back_ref, out_ref, mixed_ref, score_ref):
-    back = back_ref[...]
-    weight = weight_ref[...]
+def combine_kernel(
+    pick_ref, weight_ref, ids_ref, back_ref, out_ref, mixed_ref, score_ref, back_v, mixed_v, in_s, out_s
+):
+    ins, outs = pieces(back_ref, back_v, in_s), pieces(mixed_v, mixed_ref, out_s)
+    begin(ins)
+    weight = weight_ref[...].T
     upper = weight.astype(BF16)
     lower = (weight - upper.astype(F32)).astype(BF16)
-    mixed_ref[...] = (dot_tn(upper, back) + dot_tn(lower, back)).astype(BF16)
-    pairs = dot_nt(back, out_ref[...])
+    wide = back_v.shape[1] // PIECES
+    pairs = 0.0
+    for i in range(PIECES):
+        c = slice(i * wide, (i + 1) * wide)
+        ins[i].wait()
+        back = back_v[:, c]
+        mixed_v[:, c] = (dot_nn(upper, back) + dot_nn(lower, back)).astype(BF16)
+        outs[i].start()
+        pairs += dot_nt(back, out_ref[:, c])
     pairs = jnp.where(pick_ref[...] > 0.5, pairs, 0.0)
     queue, tok = pairs.shape
     expert = lax.broadcasted_iota(jnp.int32, (queue, tok), 0) // SLOTS
@@ -85,10 +131,45 @@
     for k in range(ids.shape[0]):
         hit = jnp.broadcast_to(ids[k : k + 1, :], (queue, tok)) == expert
         score_ref[k : k + 1, :] = jnp.sum(jnp.where(hit, pairs, 0.0), axis=0, keepdims=True)
+    finish(outs)
 
 
 def spread_kernel(pick_ref, back_ref, out_ref):
     out_ref[...] = dot_tn(pick_ref[...], back_ref[...]).astype(BF16)
+
+
+def sum_kernel(near_ref, far_ref, out_ref):
+    out_ref[...] = (near_ref[...] + far_ref[...].astype(F32)).astype(BF16)
+
+
+def columns_kernel(part_ref, own_ref, oth_ref, dg_ref, du_ref, gate_ref, up_ref):
+    def write(x):
+        turned = x.T
+        gate_ref[...] = dot_nn(turned, dg_ref[...]).astype(BF16)
+        up_ref[...] = dot_nn(turned, du_ref[...]).astype(BF16)
+
+    near = pl.program_id(0) < pl.num_programs(0) // 2
+
+    @pl.when(near)
+    def _():
+        write(own_ref[...])
+
+    @pl.when(jnp.logical_not(near))
+    def _():
+        write(oth_ref[...])
+
+
+def rows_kernel(part_ref, own_ref, oth_ref, h_ref, down_ref):
+    turned = h_ref[...].T
+    near = pl.program_id(0) < pl.num_programs(0) // 2
+
+    @pl.when(near)
+    def _():
+        down_ref[...] = dot_nn(turned, own_ref[...]).astype(BF16)
+
+    @pl.when(jnp.logical_not(near))
+    def _():
+        down_ref[...] = dot_nn(turned, oth_ref[...]).astype(BF16)
 
 
 def fetch(src, dst, sems):
@@ -186,15 +267,16 @@
     return pltpu.with_memory_space_constraint(x, pltpu.HBM)
 
 
-def call(kernel, outs, *args, specs=None, scratch=(), flops=0, mib=6):
-    shapes = [(pltpu.VMEM if kept else jax.ShapeDtypeStruct)(s, d) for s, d, kept in outs]
+def call(kernel, outs, *args, specs=None, out_specs=None, scratch=(), flops=0, mib=6):
+    kinds = {True: pltpu.VMEM, None: pltpu.HBM, False: jax.ShapeDtypeStruct}
+    shapes = [kinds[kept](s, d) for s, d, kept in outs]
     moved = sum(a.size * a.dtype.itemsize for a in args) + sum(
         math.prod(s) * jnp.dtype(d).itemsize for s, d, _ in outs
     )
     result = pl.pallas_call(
         kernel,
         in_specs=specs or [SMEM] + [VMEM] * (len(args) - 1),
-        out_specs=[VMEM] * len(shapes),
+        out_specs=out_specs or [VMEM] * len(shapes),
         out_shape=shapes,
         scratch_shapes=list(scratch),
         compiler_params=params(mib),
@@ -209,6 +291,10 @@
         specs=[ANY] * len(arrays), scratch=[DMAS] * len(arrays),
     )
     return kept
+
+
+def sems(n):
+    return pltpu.SemaphoreType.DMA((n,))
 
 
 def swap(x):
@@ -237,30 +323,17 @@
     ids_t, gates_t = expert_ids.T, gate_values.T
     unit = 2 * queue * half * hid
 
-    send, pick, weight = pl.pallas_call(
+    rows_v = pltpu.VMEM((queue, half), BF16)
+    outs_v = pltpu.VMEM((tok, half), BF16)
+    send, pick, weight = call(
         dispatch_kernel,
-        grid_spec=pltpu.PrefetchScalarGridSpec(
-            num_scalar_prefetch=1,
-            grid=(1,),
-            in_specs=[
-                pl.BlockSpec((top, tok), lambda i, s: (0, 0)),
-                pl.BlockSpec((top, tok), lambda i, s: (0, 0)),
-                pl.BlockSpec((tok, half), lambda i, s: (0, s[0])),
-            ],
-            out_specs=[
-                pl.BlockSpec((queue, half), lambda i, s: (0, 0)),
-                pl.BlockSpec((queue, tok), lambda i, s: (0, 0)),
-                pl.BlockSpec((queue, tok), lambda i, s: (0, 0)),
-            ],
-        ),
-        out_shape=[
-            jax.ShapeDtypeStruct((queue, half), BF16),
-            jax.ShapeDtypeStruct((queue, tok), BF16),
-            jax.ShapeDtypeStruct((queue, tok), F32),
-        ],
-        compiler_params=params(8),
-        name="dispatch",
-    )(jnp.concatenate([mine, tiles]), in_hbm(ids_t), in_hbm(gates_t), in_hbm(tokens))
+        [((queue, half), BF16, None), ((queue, tok), BF16, None), ((queue, tok), F32, None)],
+        mine, tiles, in_hbm(ids_t), in_hbm(gates_t), in_hbm(tokens),
+        specs=[SMEM] * 2 + [ANY] * 3, out_specs=[ANY] * 3,
+        scratch=[pltpu.VMEM((top, tok), jnp.int32), pltpu.VMEM((top, tok), F32), outs_v, rows_v]
+        + [pltpu.VMEM((queue, tok), BF16), pltpu.VMEM((queue, tok), F32), sems(4), sems(PIECES), sems(PIECES)],
+        flops=2 * queue * tok * half,
+    )
     x_own = exchange(send, experts)
     dy_send = call(
         cotangent_kernel, [((queue, half), BF16, False)], pick, weight, grad_out,
@@ -283,7 +356,7 @@
     y_far = call(leave_kernel, [((queue, half), BF16, False)], other, h, wd0, flops=unit)
     y_far = swap(y_far)
     y_near = call(leave_kernel, [((queue, half), F32, False)], mine, h, wd0, flops=unit)
-    y_sum = (y_near + y_far.astype(F32)).astype(BF16)
+    y_sum = call(sum_kernel, [((queue, half), BF16, None)], y_near, y_far, specs=[VMEM] * 2)
     y_back = exchange(y_sum, experts)
 
     dy_oth = swap(dy_own)
@@ -296,31 +369,52 @@
         inner_kernel, [((queue, hid), BF16, False)] * 2, other, dy_oth, wd1, dh0, a, b,
         flops=unit,
     )
-    dx_far = call(
-        input_kernel, [((queue, half), BF16, False)], other, dg, du, wg1, wu1, flops=2 * unit
-    )
+    dx_far = call(input_kernel, [((queue, half), BF16, False)], other, dg, du, wg1, wu1, flops=2 * unit)
     dx_far = swap(dx_far)
-    dx_near = call(
-        input_kernel, [((queue, half), F32, False)], mine, dg, du, wg1, wu1, flops=2 * unit
-    )
-    dx_sum = (dx_near + dx_far.astype(F32)).astype(BF16)
+    dx_near = call(input_kernel, [((queue, half), F32, False)], mine, dg, du, wg1, wu1, flops=2 * unit)
+    dx_sum = call(sum_kernel, [((queue, half), BF16, None)], dx_near, dx_far, specs=[VMEM] * 2)
     dx_back = exchange(dx_sum, experts)
 
-    first = me == 0
-    x_full = jnp.where(
-        first, jnp.concatenate([x_own, x_oth], 1), jnp.concatenate([x_oth, x_own], 1)
-    )
-    dy_full = jnp.where(
-        first, jnp.concatenate([dy_own, dy_oth], 1), jnp.concatenate([dy_oth, dy_own], 1)
-    )
-    grad_down = dot_tn(h, dy_full).astype(BF16)
-    grad_gate = dot_tn(x_full, dg).astype(BF16)
-    grad_up = dot_tn(x_full, du).astype(BF16)
+    blocks = 2
+    wide = half // blocks
+    keep = lambda i, s: (0, 0)
+    own = lambda i, s: (0, jnp.minimum(i, blocks - 1))
+    oth = lambda i, s: (0, jnp.maximum(i - blocks, 0))
+    place = lambda i, s: jnp.where(i < blocks, s[0] * blocks + i, (1 - s[0]) * blocks + i - blocks)
+
+    def gradients(kernel, ins, halves, whole, out_spec, shapes):
+        return pl.pallas_call(
+            kernel,
+            grid_spec=pltpu.PrefetchScalarGridSpec(
+                num_scalar_prefetch=1,
+                grid=(2 * blocks,),
+                in_specs=[pl.BlockSpec((queue, wide), own), pl.BlockSpec((queue, wide), oth)]
+                + [pl.BlockSpec((queue, hid), keep)] * len(whole),
+                out_specs=[out_spec] * len(shapes),
+            ),
+            out_shape=shapes,
+            compiler_params=params(40),
+            cost_estimate=cost(2 * unit * len(shapes), 2 * width * hid * len(shapes)),
+        )(ins, *(in_hbm(v) for v in (*halves, *whole)))
+
+    grad_gate, grad_up = gradients(
+        columns_kernel, mine, (x_own, x_oth), (dg, du),
+        pl.BlockSpec((wide, hid), lambda i, s: (place(i, s), 0)),
+        [jax.ShapeDtypeStruct((width, hid), BF16)] * 2,
+    )
+
+    (grad_down,) = gradients(
+        rows_kernel, mine, (dy_own, dy_oth), (h,),
+        pl.BlockSpec((hid, wide), lambda i, s: (0, place(i, s))),
+        [jax.ShapeDtypeStruct((hid, width), BF16)],
+    )
 
     mixed, score = call(
-        combine_kernel, [((tok, half), BF16, False), ((top, tok), F32, False)],
-        pick, weight, ids_t, y_back, grad_out,
-        specs=[VMEM] * 5, flops=6 * queue * tok * half,
+        combine_kernel, [((tok, half), BF16, None), ((top, tok), F32, False)],
+        pick, weight, ids_t, in_hbm(y_back), grad_out,
+        specs=[VMEM] * 3 + [ANY, VMEM], out_specs=[ANY, VMEM],
+        scratch=[rows_v, outs_v, sems(PIECES), sems(PIECES)],
+        mib=8, flops=6 * queue * tok * half,
     )
     grad_gates = (score + swap(score)).T
     grad_tokens = call(

time: 145 us -> 124 us (0.86)
  matrix products: 18.7 us -> 0 us
  Pallas kernels: 40 us -> 56.4 us
  local copies, waits for them, and re-layouts: 19.9 us -> 7.44 us
  other arithmetic: 4.13 us -> 0.6 us
  waiting for transfers between devices: 32.7 us -> 31.2 us
    dot_general x3 -> x0, matrix products: 18.7 us -> none  [dot_tn(): lax.dot_general(a, b, (((0,), (0,)), ((), ())), preferred_element_type=F32)]
    pallas_call x1 -> x2, Pallas kernels: 3.35 us -> 15.8 us  [gradients(): pl.pallas_call(kernel, grid_spec=pltpu.PrefetchScalarGridSpec(num_scalar_...]
    unnamed x44 -> x42, local copies, waits for them, and re-layouts: 19.9 us -> 7.44 us
    pallas_call x13 -> x16, Pallas kernels: 36.7 us -> 40.5 us  [call(): pl.pallas_call(kernel, in_specs=specs or [SMEM] + [VMEM] * (len(args) - 1...]
    convert_element_type x2 -> x0, other arithmetic: 3.46 us -> none  [the longest x1 2.3 us: paired(): y_sum = (y_near + y_far.astype(F32)).astype(BF16)]
    all_to_all x4, waiting for transfers between devices: 32.6 us -> 30.9 us  [exchange(): lax.all_to_all(x.reshape(experts, rows // experts, width), 'expert', 0, 0...]
  transfers between devices with their start and end apart: 9 -> 9, of which waited for: 4 -> 5; matrix products, arithmetic and copies ran while one was open for 16% -> 0% of each run, Pallas kernels for 25% -> 43%
where the time goes in v2:
time: 124 us; the launch traced here: 123 us
  Pallas kernels  56.4 us (45%)
  waiting for transfers between devices  31.2 us (25%)
  starting transfers between devices  25.7 us (21%)
  local copies, waits for them, and re-layouts  7.44 us (6%)
  between operations  1.67 us (1%)
    pallas_call x16, Pallas kernels, call(): pl.pallas_call(kernel, in_specs=specs or [SMEM] + [VMEM] * (len(args) - 1...  40.5 us
    all_to_all x4, waiting for transfers between devices, exchange(): lax.all_to_all(x.reshape(experts, rows // experts, width), 'expert', 0, 0...  30.9 us
    all_to_all x4, starting transfers between devices, exchange(): lax.all_to_all(x.reshape(experts, rows // experts, width), 'expert', 0, 0...  24.9 us
    pallas_call x2, Pallas kernels, gradients(): pl.pallas_call(kernel, grid_spec=pltpu.PrefetchScalarGridSpec(num_scalar_...  15.8 us
    unnamed x42, local copies, waits for them, and re-layouts  7.44 us
  transfers between devices with their start and end apart: 9, of which 5 were waited for; matrix products, arithmetic and copies ran while one was open for 0% of the time, Pallas kernels for 43%

profile of v2, /device:TPU:0, one launch (start us, length us, event | category | flops | bytes accessed | tf_op | source)
XLA Modules:
  0.0 123.0 jit_solution(16326835151659437330)
XLA Ops:
  1.3 2.6 %shard_map.127 = (bf16[256,1792]{1,0:T(8,128)(2,1)}, bf16[256,256]{1,0:T(8,128)(2,1)}, f32[256,256]{1,0:T(8,128)}) custom-call(s32[1]{0:T(128)} %bitcast.part_ref, s32[1]{0:T(128)S(6)} %copy.14.tiles_ref, s32[8,256]{1,0:T(8,128)} %bitcast.26, f32[8,256]{1,0:T(8,128)} %bitcast.39, bf16[256,3584]{1,0:T(8,128)(2,1)} %tok_ref.1), custom_call_target="tpu_custom_call" | custom-call | flops 234881024 | bytes 3162120 | tf_op jit(solution)/shard_map/pallas_call | solution.py:276
  3.9 8.4 %all-to-all-start = ((bf16[16,16,1792]{2,1,0:T(8,128)(2,1)}), bf16[16,16,1792]{2,1,0:T(8,128)(2,1)S(1)}, u32[]{:S(2)}, u32[]{:S(2)}) async-start(bf16[16,16,1792]{2,1,0:T(8,128)(2,1)} %bitcast.38), calls=%async_computation | async-start | bytes 1835008 | tf_op jit(solution)/shard_map/all_to_all | solution.py:306
  12.3 0.0 copy-start.8
  12.3 1.2 copy-done.8
  13.5 0.9 copy-done.11
  14.4 0.9 copy-done.17
  15.3 1.3 %shard_map.128 = bf16[256,1792]{1,0:T(8,128)(2,1)} custom-call(bf16[256,256]{1,0:T(8,128)(2,1)S(1)} %copy-done.11, f32[256,256]{1,0:T(8,128)S(1)} %copy-done.17, bf16[256,1792]{1,0:T(8,128)(2,1)S(1)} %copy-done.8), custom_call_target="tpu_custom_call" | custom-call | flops 234881024 | bytes 2228224 | tf_op jit(solution)/shard_map/pallas_call | solution.py:276
  16.7 17.6 %all-to-all-done = bf16[16,16,1792]{2,1,0:T(8,128)(2,1)S(1)} async-done(((bf16[16,16,1792]{2,1,0:T(8,128)(2,1)}), bf16[16,16,1792]{2,1,0:T(8,128)(2,1)S(1)}, u32[]{:S(2)}, u32[]{:S(2)}) %all-to-all-start) | async-done | bytes 917536 | tf_op jit(solution)/shard_map/all_to_all | solution.py:306
  34.3 5.5 %all-to-all-start.2 = ((bf16[16,16,1792]{2,1,0:T(8,128)(2,1)}), bf16[16,16,1792]{2,1,0:T(8,128)(2,1)S(1)}, u32[]{:S(2)}, u32[]{:S(2)}) async-start(bf16[16,16,1792]{2,1,0:T(8,128)(2,1)} %bitcast.10), calls=%async_computation.2 | async-start | bytes 1835008 | tf_op jit(solution)/shard_map/all_to_all | solution.py:306
  39.8 0.1 collective-permute-start
  39.8 5.3 %shard_map.129 = (bf16[3584,1024]{1,0:T(8,128)(2,1)S(1)}, bf16[3584,1024]{1,0:T(8,128)(2,1)S(1)}) custom-call(bf16[3584,1024]{1,0:T(8,128)(2,1)} %bitcast.30, bf16[3584,1024]{1,0:T(8,128)(2,1)} %bitcast.32), custom_call_target="tpu_custom_call" | custom-call | bytes 29360128 | tf_op jit(solution)/shard_map/pallas_call | solution.py:276
  45.2 4.6 %shard_map.130 = (f32[256,1024]{1,0:T(8,128)S(1)}, f32[256,1024]{1,0:T(8,128)S(1)}, bf16[1024,3584]{1,0:T(8,128)(2,1)S(1)}) custom-call(s32[1]{0:T(128)} %bitcast.part_ref, bf16[256,1792]{1,0:T(8,128)(2,1)S(1)} %bitcast.24, bf16[3584,1024]{1,0:T(8,128)(2,1)S(1)} %get-tuple-element.32.wg_ref, bf16[3584,1024]{1,0:T(8,128)(2,1)S(1)} %get-tuple-element.33.wu_ref, ...), custom_call_target="tpu_custom_call" | custom-call | flops 1879048192 | bytes 32374788 | tf_op jit(solution)/shard_map/pallas_call | solution.py:276
  49.8 0.0 copy-start
  49.8 2.4 %shard_map.131 = (bf16[256,1024]{1,0:T(8,128)(2,1)S(1)}, bf16[256,1024]{1,0:T(8,128)(2,1)S(1)}, bf16[256,1024]{1,0:T(8,128)(2,1)S(1)}) custom-call(s32[1]{0:T(128)S(6)} %sub.3.part_ref, bf16[256,1792]{1,0:T(8,128)(2,1)S(1)} %collective-permute-done.x_ref.oth_ref, bf16[3584,1024]{1,0:T(8,128)(2,1)S(1)} %get-tuple-element.32.wg_ref, ...), custom_call_target="tpu_custom_call" | custom-call | flops 1879048192 | bytes 19267588 | tf_op jit(solution)/shard_map/pallas_call | solution.py:276
  52.2 0.2 copy-done.10
  52.4 0.7 copy-done
  53.1 1.1 shard_map.133
  54.3 0.6 collective-permute-start.1
  54.8 5.7 %all-to-all-done.2 = bf16[16,16,1792]{2,1,0:T(8,128)(2,1)S(1)} async-done(((bf16[16,16,1792]{2,1,0:T(8,128)(2,1)}), bf16[16,16,1792]{2,1,0:T(8,128)(2,1)S(1)}, u32[]{:S(2)}, u32[]{:S(2)}) %all-to-all-start.2) | async-done | bytes 917536 | tf_op jit(solution)/shard_map/all_to_all | solution.py:306
  60.5 0.0 collective-permute-start.2
  60.5 3.4 %copy-done.1 = bf16[1024,3584]{1,0:T(8,128)(2,1)S(1)} copy-done((bf16[1024,3584]{1,0:T(8,128)(2,1)S(1)}, bf16[1024,3584]{1,0:T(8,128)(2,1)}, u32[]{:S(2)}) %copy-start.1) | copy-done | bytes 7340056
  63.9 1.1 shard_map.132.near_ref
  65.1 2.3 %shard_map.134 = bf16[256,1792]{1,0:T(8,128)(2,1)} custom-call(f32[256,1792]{1,0:T(8,128)S(1)} %shard_map.132.near_ref, bf16[256,1792]{1,0:T(8,128)(2,1)} %collective-permute-done.1.far_ref), custom_call_target="tpu_custom_call" | custom-call | bytes 3670016 | tf_op jit(solution)/shard_map/pallas_call | solution.py:276
  67.3 5.6 %all-to-all-start.1 = ((bf16[16,16,1792]{2,1,0:T(8,128)(2,1)}), bf16[16,16,1792]{2,1,0:T(8,128)(2,1)S(1)}, u32[]{:S(2)}, u32[]{:S(2)}) async-start(bf16[16,16,1792]{2,1,0:T(8,128)(2,1)} %bitcast.35), calls=%async_computation.1 | async-start | bytes 1835008 | tf_op jit(solution)/shard_map/all_to_all | solution.py:306
  72.9 3.2 %shard_map.136.w_ref = bf16[1024,3584]{1,0:T(8,128)(2,1)S(1)} custom-call(bf16[1024,3584]{1,0:T(8,128)(2,1)} %bitcast.29), custom_call_target="tpu_custom_call" | custom-call | bytes 14680064 | tf_op jit(solution)/shard_map/pallas_call | solution.py:276
  76.1 0.0 copy-start.14
  76.1 0.0 copy-start.16
  76.1 5.4 %shard_map.137 = (f32[256,1024]{1,0:T(8,128)S(1)}, bf16[3584,1024]{1,0:T(8,128)(2,1)S(1)}, bf16[3584,1024]{1,0:T(8,128)(2,1)S(1)}) custom-call(s32[1]{0:T(128)} %bitcast.part_ref, bf16[256,1792]{1,0:T(8,128)(2,1)S(1)} %bitcast.20, bf16[1024,3584]{1,0:T(8,128)(2,1)S(1)} %shard_map.136.w_ref, bf16[3584,1024]{1,0:T(8,128)(2,1)} %bitcast.31, ...), custom_call_target="tpu_custom_call" | custom-call | flops 939524096 | bytes 38666244 | tf_op jit(solution)/shard_map/pallas_call | solution.py:276
  81.5 0.0 copy-done.16
  81.6 1.2 %shard_map.138 = (bf16[256,1024]{1,0:T(8,128)(2,1)S(1)}, bf16[256,1024]{1,0:T(8,128)(2,1)S(1)}) custom-call(s32[1]{0:T(128)S(6)} %sub.3.part_ref, bf16[256,1792]{1,0:T(8,128)(2,1)S(1)} %collective-permute-done.2.dy_ref.oth_ref, bf16[1024,3584]{1,0:T(8,128)(2,1)S(1)} %shard_map.136.w_ref, f32[256,1024]{1,0:T(8,128)S(1)} %get-tuple-element.40.dh0_ref, ...), custom_call_target="tpu_custom_call" | custom-call | flops 939524096 | bytes 11403268 | tf_op jit(solution)/shard_map/pallas_call | solution.py:276
  82.8 0.0 copy-start.6
  82.8 0.0 copy-start.7
  82.8 2.1 %shard_map.140 = bf16[256,1792]{1,0:T(8,128)(2,1)S(1)} custom-call(s32[1]{0:T(128)S(6)} %sub.3.part_ref, bf16[256,1024]{1,0:T(8,128)(2,1)S(1)} %get-tuple-element.43.dg_ref, bf16[256,1024]{1,0:T(8,128)(2,1)S(1)} %get-tuple-element.44.du_ref, bf16[3584,1024]{1,0:T(8,128)(2,1)S(1)} %get-tuple-element.45.wg_ref, bf16[3584,1024]{1,0:T(8,128)(2,1)S(1)} %get-tuple-element.46.wu_ref), custom_call_target="tpu_custom_call" | custom-call | flops 1879048192 | bytes 16646148 | tf_op jit(solution)/shard_map/pallas_call | solution.py:276
  84.9 0.1 collective-permute-start.3
  85.0 2.1 %shard_map.139.near_ref = f32[256,1792]{1,0:T(8,128)S(1)} custom-call(s32[1]{0:T(128)} %bitcast.part_ref, bf16[256,1024]{1,0:T(8,128)(2,1)S(1)} %get-tuple-element.43.dg_ref, bf16[256,1024]{1,0:T(8,128)(2,1)S(1)} %get-tuple-element.44.du_ref, bf16[3584,1024]{1,0:T(8,128)(2,1)S(1)} %get-tuple-element.45.wg_ref, bf16[3584,1024]{1,0:T(8,128)(2,1)S(1)} %get-tuple-element.46.wu_ref), custom_call_target="tpu_custom_call" | custom-call | flops 1879048192 | bytes 17563652 | tf_op jit(solution)/shard_map/pallas_call | solution.py:276
  87.1 0.3 collective-permute-done.3.far_ref
  87.5 1.1 shard_map.141
  88.5 6.7 %all-to-all-done.1 = bf16[16,16,1792]{2,1,0:T(8,128)(2,1)S(1)} async-done(((bf16[16,16,1792]{2,1,0:T(8,128)(2,1)}), bf16[16,16,1792]{2,1,0:T(8,128)(2,1)S(1)}, u32[]{:S(2)}, u32[]{:S(2)}) %all-to-all-start.1) | async-done | bytes 917536 | tf_op jit(solution)/shard_map/all_to_all | solution.py:306
  95.2 5.5 %all-to-all-start.3 = ((bf16[16,16,1792]{2,1,0:T(8,128)(2,1)}), bf16[16,16,1792]{2,1,0:T(8,128)(2,1)S(1)}, u32[]{:S(2)}, u32[]{:S(2)}) async-start(bf16[16,16,1792]{2,1,0:T(8,128)(2,1)} %bitcast.36), calls=%async_computation.3 | async-start | bytes 1835008 | tf_op jit(solution)/shard_map/all_to_all | solution.py:306
  100.8 0.0 copy-start.9
  100.8 0.0 copy-start.19
  100.8 8.9 %shard_map.143 = (bf16[3584,1024]{1,0:T(8,128)(2,1)}, bf16[3584,1024]{1,0:T(8,128)(2,1)}) custom-call(s32[1]{0:T(128)} %bitcast.part_ref, bf16[256,1792]{1,0:T(8,128)(2,1)} %bitcast.25, bf16[256,1792]{1,0:T(8,128)(2,1)} %copy-done.10, bf16[256,1024]{1,0:T(8,128)(2,1)} %copy-done.6, bf16[256,1024]{1,0:T(8,128)(2,1)} %copy-done.7), custom_call_target="tpu_custom_call" | custom-call | flops 3758096384 | bytes 14680064 | tf_op jit(solution)/shard_map/pallas_call | solution.py:386
  109.7 3.3 %shard_map.135 = (bf16[256,1792]{1,0:T(8,128)(2,1)}, f32[8,256]{1,0:T(8,128)S(1)}) custom-call(bf16[256,256]{1,0:T(8,128)(2,1)S(1)} %copy-done.12, f32[256,256]{1,0:T(8,128)S(1)} %copy-done.18, s32[8,256]{1,0:T(8,128)S(1)} %bitcast.27, bf16[256,1792]{1,0:T(8,128)(2,1)} %bitcast.37, bf16[256,1792]{1,0:T(8,128)(2,1)S(1)} %copy-done.9), custom_call_target="tpu_custom_call" | custom-call | flops 704643072 | bytes 3162112 | tf_op jit(solution)/shard_map/pallas_call | solution.py:276
  113.0 0.1 collective-permute-start.4
  113.1 7.0 %shard_map.144 = bf16[1024,3584]{1,0:T(8,128)(2,1)} custom-call(s32[1]{0:T(128)} %bitcast.part_ref, bf16[256,1792]{1,0:T(8,128)(2,1)} %bitcast.21, bf16[256,1792]{1,0:T(8,128)(2,1)} %copy-done.4, bf16[256,1024]{1,0:T(8,128)(2,1)} %copy-done.3), custom_call_target="tpu_custom_call" | custom-call | flops 1879048192 | bytes 7340032 | tf_op jit(solution)/shard_map/pallas_call | solution.py:386
  120.1 0.6 add_bitcast_fusion
  120.7 1.0 all-to-all-done.3
  121.7 1.4 %shard_map.142 = bf16[256,1792]{1,0:T(8,128)(2,1)} custom-call(bf16[256,256]{1,0:T(8,128)(2,1)S(1)} %copy-done.12, bf16[256,1792]{1,0:T(8,128)(2,1)S(1)} %bitcast.22), custom_call_target="tpu_custom_call" | custom-call | flops 234881024 | bytes 1966080 | tf_op jit(solution)/shard_map/pallas_call | solution.py:276
  (31 shorter events, 0.1 us)
Async XLA Ops:
  3.9 30.3 %all-to-all-start = ((bf16[16,16,1792]{2,1,0:T(8,128)(2,1)}), bf16[16,16,1792]{2,1,0:T(8,128)(2,1)S(1)}, u32[]{:S(2)}, u32[]{:S(2)}) async-start(bf16[16,16,1792]{2,1,0:T(8,128)(2,1)} %bitcast.38), calls=%async_computation | async-start | bytes 1835008 | tf_op jit(solution)/shard_map/all_to_all | solution.py:306
  12.3 1.2 copy-start.8
  13.5 0.9 copy-start.11
  14.4 0.9 copy-start.17
  34.3 10.9 %copy-start.5 = (bf16[16,16,1792]{2,1,0:T(8,128)(2,1)}, bf16[16,16,1792]{2,1,0:T(8,128)(2,1)S(1)}, u32[]{:S(2)}) copy-start(bf16[16,16,1792]{2,1,0:T(8,128)(2,1)S(1)} %all-to-all-done) | copy-start | bytes 2752516
  34.3 26.2 %all-to-all-start.2 = ((bf16[16,16,1792]{2,1,0:T(8,128)(2,1)}), bf16[16,16,1792]{2,1,0:T(8,128)(2,1)S(1)}, u32[]{:S(2)}, u32[]{:S(2)}) async-start(bf16[16,16,1792]{2,1,0:T(8,128)(2,1)} %bitcast.10), calls=%async_computation.2 | async-start | bytes 1835008 | tf_op jit(solution)/shard_map/all_to_all | solution.py:306
  39.8 10.0 %collective-permute-start = (bf16[256,1792]{1,0:T(8,128)(2,1)S(1)}, bf16[256,1792]{1,0:T(8,128)(2,1)S(1)}, u32[]{:S(2)}, u32[]{:S(2)}) collective-permute-start(bf16[256,1792]{1,0:T(8,128)(2,1)S(1)} %bitcast.23), channel_id=1, source_target_pairs={{0,1},{1,0},{2,3},{3,2},{4,5},{5,4},{6,7},{7,6},{8,9},{9,8},{10,11... | collective-permute-start | bytes 2752520 | tf_op jit(solution)/shard_map/ppermute | solution.py:301
  49.8 3.3 %copy-start = (bf16[1024,3584]{1,0:T(8,128)(2,1)}, bf16[1024,3584]{1,0:T(8,128)(2,1)S(1)}, u32[]{:S(2)}) copy-start(bf16[1024,3584]{1,0:T(8,128)(2,1)S(1)} %get-tuple-element.37.w_ref) | copy-start | bytes 22020100
  49.8 2.6 %copy-start.10 = (bf16[256,1792]{1,0:T(8,128)(2,1)}, bf16[256,1792]{1,0:T(8,128)(2,1)S(1)}, u32[]{:S(2)}) copy-start(bf16[256,1792]{1,0:T(8,128)(2,1)S(1)} %collective-permute-done.x_ref.oth_ref) | copy-start | bytes 2752516
  52.4 1.9 %copy-start.13 = (bf16[256,1024]{1,0:T(8,128)(2,1)}, bf16[256,1024]{1,0:T(8,128)(2,1)S(1)}, u32[]{:S(2)}) copy-start(bf16[256,1024]{1,0:T(8,128)(2,1)S(1)} %get-tuple-element.41.a_ref) | copy-start | bytes 1572868
  52.4 1.9 %copy-start.15 = (bf16[256,1024]{1,0:T(8,128)(2,1)}, bf16[256,1024]{1,0:T(8,128)(2,1)S(1)}, u32[]{:S(2)}) copy-start(bf16[256,1024]{1,0:T(8,128)(2,1)S(1)} %get-tuple-element.42.b_ref) | copy-start | bytes 1572868
  52.4 12.7 %copy-start.3 = (bf16[256,1024]{1,0:T(8,128)(2,1)}, bf16[256,1024]{1,0:T(8,128)(2,1)S(1)}, u32[]{:S(2)}) copy-start(bf16[256,1024]{1,0:T(8,128)(2,1)S(1)} %get-tuple-element.36.h_ref) | copy-start | bytes 1572868
  54.3 10.8 %collective-permute-start.1 = (bf16[256,1792]{1,0:T(8,128)(2,1)S(1)}, bf16[256,1792]{1,0:T(8,128)(2,1)}, u32[]{:S(2)}, u32[]{:S(2)}) collective-permute-start(bf16[256,1792]{1,0:T(8,128)(2,1)S(1)} %shard_map.133), channel_id=1, source_target_pairs={{0,1},{1,0},{2,3},{3,2},{4,5},{5,4},{6,7},{7,6},{8,9},{9,8},{10,11... | collective-permute-start | bytes 2752520 | tf_op jit(solution)/shard_map/ppermute | solution.py:301
  60.5 15.6 %copy-start.2 = (bf16[16,16,1792]{2,1,0:T(8,128)(2,1)}, bf16[16,16,1792]{2,1,0:T(8,128)(2,1)S(1)}, u32[]{:S(2)}) copy-start(bf16[16,16,1792]{2,1,0:T(8,128)(2,1)S(1)} %all-to-all-done.2) | copy-start | bytes 2752516
  60.5 21.0 %collective-permute-start.2 = (bf16[256,1792]{1,0:T(8,128)(2,1)S(1)}, bf16[256,1792]{1,0:T(8,128)(2,1)S(1)}, u32[]{:S(2)}, u32[]{:S(2)}) collective-permute-start(bf16[256,1792]{1,0:T(8,128)(2,1)S(1)} %bitcast.19), channel_id=1, source_target_pairs={{0,1},{1,0},{2,3},{3,2},{4,5},{5,4},{6,7},{7,6},{8,9},{9,8},{10,11... | collective-permute-start | bytes 2752520 | tf_op jit(solution)/shard_map/ppermute | solution.py:301
  60.5 3.4 %copy-start.1 = (bf16[1024,3584]{1,0:T(8,128)(2,1)S(1)}, bf16[1024,3584]{1,0:T(8,128)(2,1)}, u32[]{:S(2)}) copy-start(bf16[1024,3584]{1,0:T(8,128)(2,1)} %copy-done) | copy-start | bytes 22020100
  67.3 27.9 %all-to-all-start.1 = ((bf16[16,16,1792]{2,1,0:T(8,128)(2,1)}), bf16[16,16,1792]{2,1,0:T(8,128)(2,1)S(1)}, u32[]{:S(2)}, u32[]{:S(2)}) async-start(bf16[16,16,1792]{2,1,0:T(8,128)(2,1)} %bitcast.35), calls=%async_computation.1 | async-start | bytes 1835008 | tf_op jit(solution)/shard_map/all_to_all | solution.py:306
  76.1 5.4 %copy-start.14 = (bf16[256,1024]{1,0:T(8,128)(2,1)S(1)}, bf16[256,1024]{1,0:T(8,128)(2,1)}, u32[]{:S(2)}) copy-start(bf16[256,1024]{1,0:T(8,128)(2,1)} %copy-done.13) | copy-start | bytes 1572868
  76.1 5.4 %copy-start.16 = (bf16[256,1024]{1,0:T(8,128)(2,1)S(1)}, bf16[256,1024]{1,0:T(8,128)(2,1)}, u32[]{:S(2)}) copy-start(bf16[256,1024]{1,0:T(8,128)(2,1)} %copy-done.15) | copy-start | bytes 1572868
  81.5 3.4 %copy-start.4 = (bf16[256,1792]{1,0:T(8,128)(2,1)}, bf16[256,1792]{1,0:T(8,128)(2,1)S(1)}, u32[]{:S(2)}) copy-start(bf16[256,1792]{1,0:T(8,128)(2,1)S(1)} %collective-permute-done.2.dy_ref.oth_ref) | copy-start | bytes 2752516
  82.8 2.2 %copy-start.6 = (bf16[256,1024]{1,0:T(8,128)(2,1)}, bf16[256,1024]{1,0:T(8,128)(2,1)S(1)}, u32[]{:S(2)}) copy-start(bf16[256,1024]{1,0:T(8,128)(2,1)S(1)} %get-tuple-element.43.dg_ref) | copy-start | bytes 1572868
  82.8 2.2 %copy-start.7 = (bf16[256,1024]{1,0:T(8,128)(2,1)}, bf16[256,1024]{1,0:T(8,128)(2,1)S(1)}, u32[]{:S(2)}) copy-start(bf16[256,1024]{1,0:T(8,128)(2,1)S(1)} %get-tuple-element.44.du_ref) | copy-start | bytes 1572868
  84.9 2.5 %collective-permute-start.3 = (bf16[256,1792]{1,0:T(8,128)(2,1)S(1)}, bf16[256,1792]{1,0:T(8,128)(2,1)S(1)}, u32[]{:S(2)}, u32[]{:S(2)}) collective-permute-start(bf16[256,1792]{1,0:T(8,128)(2,1)S(1)} %shard_map.140), channel_id=1, source_target_pairs={{0,1},{1,0},{2,3},{3,2},{4,5},{5,4},{6,7},{7,6},{8,9},{9,8},{10,11... | collective-permute-start | bytes 2752520 | tf_op jit(solution)/shard_map/ppermute | solution.py:301
  95.2 14.4 %copy-start.20 = (bf16[16,16,1792]{2,1,0:T(8,128)(2,1)}, bf16[16,16,1792]{2,1,0:T(8,128)(2,1)S(1)}, u32[]{:S(2)}) copy-start(bf16[16,16,1792]{2,1,0:T(8,128)(2,1)S(1)} %all-to-all-done.1) | copy-start | bytes 2752516
  95.2 26.4 %all-to-all-start.3 = ((bf16[16,16,1792]{2,1,0:T(8,128)(2,1)}), bf16[16,16,1792]{2,1,0:T(8,128)(2,1)S(1)}, u32[]{:S(2)}, u32[]{:S(2)}) async-start(bf16[16,16,1792]{2,1,0:T(8,128)(2,1)} %bitcast.36), calls=%async_computation.3 | async-start | bytes 1835008 | tf_op jit(solution)/shard_map/all_to_all | solution.py:306
  100.8 8.9 %copy-start.9 = (bf16[256,1792]{1,0:T(8,128)(2,1)S(1)}, bf16[256,1792]{1,0:T(8,128)(2,1)}, u32[]{:S(2)}) copy-start(bf16[256,1792]{1,0:T(8,128)(2,1)} %out_ref.3) | copy-start | bytes 2752516
  100.8 8.9 %copy-start.12 = (bf16[256,256]{1,0:T(8,128)(2,1)S(1)}, bf16[256,256]{1,0:T(8,128)(2,1)}, u32[]{:S(2)}) copy-start(bf16[256,256]{1,0:T(8,128)(2,1)} %get-tuple-element.28.pick_ref) | copy-start | bytes 393220
  100.8 8.9 %copy-start.18 = (f32[256,256]{1,0:T(8,128)S(1)}, f32[256,256]{1,0:T(8,128)}, u32[]{:S(2)}) copy-start(f32[256,256]{1,0:T(8,128)} %get-tuple-element.29.weight_ref) | copy-start | bytes 786436
  100.8 8.9 %copy-start.19 = (s32[256,8]{0,1:T(8,128)S(1)}, s32[256,8]{0,1:T(8,128)}, u32[]{:S(2)}) copy-start(s32[256,8]{0,1:T(8,128)} %param.9) | copy-start | bytes 24580
  113.0 7.1 %collective-permute-start.4 = (f32[8,256]{1,0:T(8,128)S(1)}, f32[8,256]{1,0:T(8,128)S(1)}, u32[]{:S(2)}, u32[]{:S(2)}) collective-permute-start(f32[8,256]{1,0:T(8,128)S(1)} %get-tuple-element.47), channel_id=1, source_target_pairs={{0,1},{1,0},{2,3},{3,2},{4,5},{5,4},{6,7},{7,6},{8,9},{9,8},{10,11... | collective-permute-start | bytes 24584 | tf_op jit(solution)/shard_map/ppermute | solution.py:301

commit v3 on v2

--- a/solution.py
+++ b/solution.py
@@ -108,7 +108,8 @@
 
 
 def combine_kernel(
-    pick_ref, weight_ref, ids_ref, back_ref, out_ref, mixed_ref, score_ref, back_v, mixed_v, in_s, out_s
+    pick_ref, weight_ref, ids_ref, back_ref, out_ref, mixed_ref, score_ref, turned_ref,
+    back_v, mixed_v, in_s, out_s,
 ):
     ins, outs = pieces(back_ref, back_v, in_s), pieces(mixed_v, mixed_ref, out_s)
     begin(ins)
@@ -124,7 +125,9 @@
         mixed_v[:, c] = (dot_nn(upper, back) + dot_nn(lower, back)).astype(BF16)
         outs[i].start()
         pairs += dot_nt(back, out_ref[:, c])
-    pairs = jnp.where(pick_ref[...] > 0.5, pairs, 0.0)
+    pick = pick_ref[...].astype(F32)
+    turned_ref[...] = pick.T.astype(BF16)
+    pairs = jnp.where(pick > 0.5, pairs, 0.0)
     queue, tok = pairs.shape
     expert = lax.broadcasted_iota(jnp.int32, (queue, tok), 0) // SLOTS
     ids = ids_ref[...]
@@ -134,8 +137,14 @@
     finish(outs)
 
 
-def spread_kernel(pick_ref, back_ref, out_ref):
-    out_ref[...] = dot_tn(pick_ref[...], back_ref[...]).astype(BF16)
+def spread_kernel(turned_ref, back_ref, out_ref, out_v, out_s):
+    outs = pieces(out_v, out_ref, out_s)
+    wide = out_v.shape[1] // PIECES
+    for i in range(PIECES):
+        c = slice(i * wide, (i + 1) * wide)
+        out_v[:, c] = dot_nn(turned_ref[...], back_ref[:, c]).astype(BF16)
+        outs[i].start()
+    finish(outs)
 
 
 def sum_kernel(near_ref, far_ref, out_ref):
@@ -409,17 +418,19 @@
         [jax.ShapeDtypeStruct((hid, width), BF16)],
     )
 
-    mixed, score = call(
-        combine_kernel, [((tok, half), BF16, None), ((top, tok), F32, False)],
+    mixed, score, turned = call(
+        combine_kernel,
+        [((tok, half), BF16, None), ((top, tok), F32, False), ((tok, queue), BF16, False)],
         pick, weight, ids_t, in_hbm(y_back), grad_out,
-        specs=[VMEM] * 3 + [ANY, VMEM], out_specs=[ANY, VMEM],
+        specs=[VMEM] * 3 + [ANY, VMEM], out_specs=[ANY, VMEM, VMEM],
         scratch=[rows_v, outs_v, sems(PIECES), sems(PIECES)],
         mib=8, flops=6 * queue * tok * half,
     )
     grad_gates = (score + swap(score)).T
     grad_tokens = call(
-        spread_kernel, [((tok, half), BF16, False)], pick, dx_back,
-        specs=[VMEM] * 2, flops=2 * queue * tok * half,
+        spread_kernel, [((tok, half), BF16, None)], turned, dx_back,
+        specs=[VMEM] * 2, out_specs=[ANY], scratch=[outs_v, sems(PIECES)],
+        flops=2 * queue * tok * half,
     )
     return mixed, grad_tokens, grad_gates, grad_gate[None], grad_up[None], grad_down[None]
 

time: 124 us -> 124 us (level)
  no operation moved by 1% of the time
where the time goes in v3:
time: 124 us; the launch traced here: 123 us
  Pallas kernels  56.2 us (45%)
  waiting for transfers between devices  31.2 us (25%)
  starting transfers between devices  25.7 us (21%)
  local copies, waits for them, and re-layouts  7.44 us (6%)
  between operations  1.83 us (1%)
    pallas_call x16, Pallas kernels, call(): pl.pallas_call(kernel, in_specs=specs or [SMEM] + [VMEM] * (len(args) - 1...  40.4 us
    all_to_all x4, waiting for transfers between devices, exchange(): lax.all_to_all(x.reshape(experts, rows // experts, width), 'expert', 0, 0...  30.9 us
    all_to_all x4, starting transfers between devices, exchange(): lax.all_to_all(x.reshape(experts, rows // experts, width), 'expert', 0, 0...  24.9 us
    pallas_call x2, Pallas kernels, gradients(): pl.pallas_call(kernel, grid_spec=pltpu.PrefetchScalarGridSpec(num_scalar_...  15.8 us
    unnamed x42, local copies, waits for them, and re-layouts  7.44 us
  transfers between devices with their start and end apart: 9, of which 5 were waited for; matrix products, arithmetic and copies ran while one was open for 0% of the time, Pallas kernels for 43%

profile of v3, /device:TPU:0, one launch (start us, length us, event | category | flops | bytes accessed | tf_op | source)
XLA Modules:
  0.0 123.1 jit_solution(16330429796101260215)
XLA Ops:
  1.3 2.6 %shard_map.127 = (bf16[256,1792]{1,0:T(8,128)(2,1)}, bf16[256,256]{1,0:T(8,128)(2,1)}, f32[256,256]{1,0:T(8,128)}) custom-call(s32[1]{0:T(128)} %bitcast.part_ref, s32[1]{0:T(128)S(6)} %copy.14.tiles_ref, s32[8,256]{1,0:T(8,128)} %bitcast.26, f32[8,256]{1,0:T(8,128)} %bitcast.39, bf16[256,3584]{1,0:T(8,128)(2,1)} %tok_ref.1), custom_call_target="tpu_custom_call" | custom-call | flops 234881024 | bytes 3162120 | tf_op jit(solution)/shard_map/pallas_call | solution.py:285
  3.9 8.4 %all-to-all-start = ((bf16[16,16,1792]{2,1,0:T(8,128)(2,1)}), bf16[16,16,1792]{2,1,0:T(8,128)(2,1)S(1)}, u32[]{:S(2)}, u32[]{:S(2)}) async-start(bf16[16,16,1792]{2,1,0:T(8,128)(2,1)} %bitcast.38), calls=%async_computation | async-start | bytes 1835008 | tf_op jit(solution)/shard_map/all_to_all | solution.py:315
  12.3 0.0 copy-start.8
  12.3 1.2 copy-done.8
  13.5 0.9 copy-done.15
  14.4 0.9 copy-done.17
  15.3 1.3 %shard_map.128 = bf16[256,1792]{1,0:T(8,128)(2,1)} custom-call(bf16[256,256]{1,0:T(8,128)(2,1)S(1)} %copy-done.17, f32[256,256]{1,0:T(8,128)S(1)} %copy-done.15, bf16[256,1792]{1,0:T(8,128)(2,1)S(1)} %copy-done.8), custom_call_target="tpu_custom_call" | custom-call | flops 234881024 | bytes 2228224 | tf_op jit(solution)/shard_map/pallas_call | solution.py:285
  16.7 17.6 %all-to-all-done = bf16[16,16,1792]{2,1,0:T(8,128)(2,1)S(1)} async-done(((bf16[16,16,1792]{2,1,0:T(8,128)(2,1)}), bf16[16,16,1792]{2,1,0:T(8,128)(2,1)S(1)}, u32[]{:S(2)}, u32[]{:S(2)}) %all-to-all-start) | async-done | bytes 917536 | tf_op jit(solution)/shard_map/all_to_all | solution.py:315
  34.3 5.5 %all-to-all-start.2 = ((bf16[16,16,1792]{2,1,0:T(8,128)(2,1)}), bf16[16,16,1792]{2,1,0:T(8,128)(2,1)S(1)}, u32[]{:S(2)}, u32[]{:S(2)}) async-start(bf16[16,16,1792]{2,1,0:T(8,128)(2,1)} %bitcast.10), calls=%async_computation.2 | async-start | bytes 1835008 | tf_op jit(solution)/shard_map/all_to_all | solution.py:315
  39.8 0.1 collective-permute-start
  39.8 5.3 %shard_map.129 = (bf16[3584,1024]{1,0:T(8,128)(2,1)S(1)}, bf16[3584,1024]{1,0:T(8,128)(2,1)S(1)}) custom-call(bf16[3584,1024]{1,0:T(8,128)(2,1)} %bitcast.30, bf16[3584,1024]{1,0:T(8,128)(2,1)} %bitcast.32), custom_call_target="tpu_custom_call" | custom-call | bytes 29360128 | tf_op jit(solution)/shard_map/pallas_call | solution.py:285
  45.2 4.6 %shard_map.130 = (f32[256,1024]{1,0:T(8,128)S(1)}, f32[256,1024]{1,0:T(8,128)S(1)}, bf16[1024,3584]{1,0:T(8,128)(2,1)S(1)}) custom-call(s32[1]{0:T(128)} %bitcast.part_ref, bf16[256,1792]{1,0:T(8,128)(2,1)S(1)} %bitcast.24, bf16[3584,1024]{1,0:T(8,128)(2,1)S(1)} %get-tuple-element.33.wg_ref, bf16[3584,1024]{1,0:T(8,128)(2,1)S(1)} %get-tuple-element.34.wu_ref, ...), custom_call_target="tpu_custom_call" | custom-call | flops 1879048192 | bytes 32374788 | tf_op jit(solution)/shard_map/pallas_call | solution.py:285
  49.8 0.0 copy-start
  49.8 2.4 %shard_map.131 = (bf16[256,1024]{1,0:T(8,128)(2,1)S(1)}, bf16[256,1024]{1,0:T(8,128)(2,1)S(1)}, bf16[256,1024]{1,0:T(8,128)(2,1)S(1)}) custom-call(s32[1]{0:T(128)S(6)} %sub.3.part_ref, bf16[256,1792]{1,0:T(8,128)(2,1)S(1)} %collective-permute-done.x_ref.oth_ref, bf16[3584,1024]{1,0:T(8,128)(2,1)S(1)} %get-tuple-element.33.wg_ref, ...), custom_call_target="tpu_custom_call" | custom-call | flops 1879048192 | bytes 19267588 | tf_op jit(solution)/shard_map/pallas_call | solution.py:285
  52.2 0.2 copy-done.10
  52.4 0.7 copy-done
  53.1 1.1 shard_map.133
  54.3 0.6 collective-permute-start.1
  54.8 5.7 %all-to-all-done.2 = bf16[16,16,1792]{2,1,0:T(8,128)(2,1)S(1)} async-done(((bf16[16,16,1792]{2,1,0:T(8,128)(2,1)}), bf16[16,16,1792]{2,1,0:T(8,128)(2,1)S(1)}, u32[]{:S(2)}, u32[]{:S(2)}) %all-to-all-start.2) | async-done | bytes 917536 | tf_op jit(solution)/shard_map/all_to_all | solution.py:315
  60.5 0.0 collective-permute-start.2
  60.5 3.4 %copy-done.1 = bf16[1024,3584]{1,0:T(8,128)(2,1)S(1)} copy-done((bf16[1024,3584]{1,0:T(8,128)(2,1)S(1)}, bf16[1024,3584]{1,0:T(8,128)(2,1)}, u32[]{:S(2)}) %copy-start.1) | copy-done | bytes 7340056
  63.9 1.1 shard_map.132.near_ref
  65.1 2.3 %shard_map.134 = bf16[256,1792]{1,0:T(8,128)(2,1)} custom-call(f32[256,1792]{1,0:T(8,128)S(1)} %shard_map.132.near_ref, bf16[256,1792]{1,0:T(8,128)(2,1)} %collective-permute-done.1.far_ref), custom_call_target="tpu_custom_call" | custom-call | bytes 3670016 | tf_op jit(solution)/shard_map/pallas_call | solution.py:285
  67.3 5.6 %all-to-all-start.1 = ((bf16[16,16,1792]{2,1,0:T(8,128)(2,1)}), bf16[16,16,1792]{2,1,0:T(8,128)(2,1)S(1)}, u32[]{:S(2)}, u32[]{:S(2)}) async-start(bf16[16,16,1792]{2,1,0:T(8,128)(2,1)} %bitcast.35), calls=%async_computation.1 | async-start | bytes 1835008 | tf_op jit(solution)/shard_map/all_to_all | solution.py:315
  72.9 3.2 %shard_map.136.w_ref = bf16[1024,3584]{1,0:T(8,128)(2,1)S(1)} custom-call(bf16[1024,3584]{1,0:T(8,128)(2,1)} %bitcast.29), custom_call_target="tpu_custom_call" | custom-call | bytes 14680064 | tf_op jit(solution)/shard_map/pallas_call | solution.py:285
  76.1 0.0 copy-start.12
  76.1 0.0 copy-start.14
  76.1 5.4 %shard_map.137 = (f32[256,1024]{1,0:T(8,128)S(1)}, bf16[3584,1024]{1,0:T(8,128)(2,1)S(1)}, bf16[3584,1024]{1,0:T(8,128)(2,1)S(1)}) custom-call(s32[1]{0:T(128)} %bitcast.part_ref, bf16[256,1792]{1,0:T(8,128)(2,1)S(1)} %bitcast.20, bf16[1024,3584]{1,0:T(8,128)(2,1)S(1)} %shard_map.136.w_ref, bf16[3584,1024]{1,0:T(8,128)(2,1)} %bitcast.31, ...), custom_call_target="tpu_custom_call" | custom-call | flops 939524096 | bytes 38666244 | tf_op jit(solution)/shard_map/pallas_call | solution.py:285
  81.5 0.0 copy-done.14
  81.6 1.2 %shard_map.138 = (bf16[256,1024]{1,0:T(8,128)(2,1)S(1)}, bf16[256,1024]{1,0:T(8,128)(2,1)S(1)}) custom-call(s32[1]{0:T(128)S(6)} %sub.3.part_ref, bf16[256,1792]{1,0:T(8,128)(2,1)S(1)} %collective-permute-done.2.dy_ref.oth_ref, bf16[1024,3584]{1,0:T(8,128)(2,1)S(1)} %shard_map.136.w_ref, f32[256,1024]{1,0:T(8,128)S(1)} %get-tuple-element.42.dh0_ref, ...), custom_call_target="tpu_custom_call" | custom-call | flops 939524096 | bytes 11403268 | tf_op jit(solution)/shard_map/pallas_call | solution.py:285
  82.8 0.0 copy-start.6
  82.8 0.0 copy-start.7
  82.8 2.1 %shard_map.140 = bf16[256,1792]{1,0:T(8,128)(2,1)S(1)} custom-call(s32[1]{0:T(128)S(6)} %sub.3.part_ref, bf16[256,1024]{1,0:T(8,128)(2,1)S(1)} %get-tuple-element.45.dg_ref, bf16[256,1024]{1,0:T(8,128)(2,1)S(1)} %get-tuple-element.46.du_ref, bf16[3584,1024]{1,0:T(8,128)(2,1)S(1)} %get-tuple-element.47.wg_ref, bf16[3584,1024]{1,0:T(8,128)(2,1)S(1)} %get-tuple-element.48.wu_ref), custom_call_target="tpu_custom_call" | custom-call | flops 1879048192 | bytes 16646148 | tf_op jit(solution)/shard_map/pallas_call | solution.py:285
  84.9 0.1 collective-permute-start.3
  85.0 2.1 %shard_map.139.near_ref = f32[256,1792]{1,0:T(8,128)S(1)} custom-call(s32[1]{0:T(128)} %bitcast.part_ref, bf16[256,1024]{1,0:T(8,128)(2,1)S(1)} %get-tuple-element.45.dg_ref, bf16[256,1024]{1,0:T(8,128)(2,1)S(1)} %get-tuple-element.46.du_ref, bf16[3584,1024]{1,0:T(8,128)(2,1)S(1)} %get-tuple-element.47.wg_ref, bf16[3584,1024]{1,0:T(8,128)(2,1)S(1)} %get-tuple-element.48.wu_ref), custom_call_target="tpu_custom_call" | custom-call | flops 1879048192 | bytes 17563652 | tf_op jit(solution)/shard_map/pallas_call | solution.py:285
  87.1 0.3 collective-permute-done.3.far_ref
  87.5 1.1 shard_map.141
  88.5 6.7 %all-to-all-done.1 = bf16[16,16,1792]{2,1,0:T(8,128)(2,1)S(1)} async-done(((bf16[16,16,1792]{2,1,0:T(8,128)(2,1)}), bf16[16,16,1792]{2,1,0:T(8,128)(2,1)S(1)}, u32[]{:S(2)}, u32[]{:S(2)}) %all-to-all-start.1) | async-done | bytes 917536 | tf_op jit(solution)/shard_map/all_to_all | solution.py:315
  95.2 5.5 %all-to-all-start.3 = ((bf16[16,16,1792]{2,1,0:T(8,128)(2,1)}), bf16[16,16,1792]{2,1,0:T(8,128)(2,1)S(1)}, u32[]{:S(2)}, u32[]{:S(2)}) async-start(bf16[16,16,1792]{2,1,0:T(8,128)(2,1)} %bitcast.36), calls=%async_computation.3 | async-start | bytes 1835008 | tf_op jit(solution)/shard_map/all_to_all | solution.py:315
  100.8 0.0 copy-start.9
  100.8 0.0 copy-start.19
  100.8 8.9 %shard_map.143 = (bf16[3584,1024]{1,0:T(8,128)(2,1)}, bf16[3584,1024]{1,0:T(8,128)(2,1)}) custom-call(s32[1]{0:T(128)} %bitcast.part_ref, bf16[256,1792]{1,0:T(8,128)(2,1)} %bitcast.25, bf16[256,1792]{1,0:T(8,128)(2,1)} %copy-done.10, bf16[256,1024]{1,0:T(8,128)(2,1)} %copy-done.6, bf16[256,1024]{1,0:T(8,128)(2,1)} %copy-done.7), custom_call_target="tpu_custom_call" | custom-call | flops 3758096384 | bytes 14680064 | tf_op jit(solution)/shard_map/pallas_call | solution.py:395
  109.7 3.3 %shard_map.135 = (bf16[256,1792]{1,0:T(8,128)(2,1)}, f32[8,256]{1,0:T(8,128)S(1)}, bf16[256,256]{1,0:T(8,128)(2,1)S(1)}) custom-call(bf16[256,256]{1,0:T(8,128)(2,1)S(1)} %copy-done.18, f32[256,256]{1,0:T(8,128)S(1)} %copy-done.16, s32[8,256]{1,0:T(8,128)S(1)} %bitcast.27, bf16[256,1792]{1,0:T(8,128)(2,1)} %bitcast.37, bf16[256,1792]{1,0:T(8,128)(2,1)S(1)} %copy-done.9), custom_call_target="tpu_custom_call" | custom-call | flops 704643072 | bytes 3293184 | tf_op jit(solution)/shard_map/pallas_call | solution.py:285
  113.0 0.1 collective-permute-start.4
  113.1 7.0 %shard_map.144 = bf16[1024,3584]{1,0:T(8,128)(2,1)} custom-call(s32[1]{0:T(128)} %bitcast.part_ref, bf16[256,1792]{1,0:T(8,128)(2,1)} %bitcast.21, bf16[256,1792]{1,0:T(8,128)(2,1)} %copy-done.4, bf16[256,1024]{1,0:T(8,128)(2,1)} %copy-done.3), custom_call_target="tpu_custom_call" | custom-call | flops 1879048192 | bytes 7340032 | tf_op jit(solution)/shard_map/pallas_call | solution.py:395
  120.1 0.6 add_bitcast_fusion
  120.7 1.0 all-to-all-done.3
  121.7 1.2 %shard_map.142 = bf16[256,1792]{1,0:T(8,128)(2,1)} custom-call(bf16[256,256]{1,0:T(8,128)(2,1)S(1)} %get-tuple-element.40.turned_ref, bf16[256,1792]{1,0:T(8,128)(2,1)S(1)} %bitcast.22), custom_call_target="tpu_custom_call" | custom-call | flops 234881024 | bytes 1966080 | tf_op jit(solution)/shard_map/pallas_call | solution.py:285
  (31 shorter events, 0.1 us)
Async XLA Ops:
  3.9 30.3 %all-to-all-start = ((bf16[16,16,1792]{2,1,0:T(8,128)(2,1)}), bf16[16,16,1792]{2,1,0:T(8,128)(2,1)S(1)}, u32[]{:S(2)}, u32[]{:S(2)}) async-start(bf16[16,16,1792]{2,1,0:T(8,128)(2,1)} %bitcast.38), calls=%async_computation | async-start | bytes 1835008 | tf_op jit(solution)/shard_map/all_to_all | solution.py:315
  12.3 1.2 copy-start.8
  13.5 0.9 copy-start.15
  14.4 0.9 copy-start.17
  34.3 10.9 %copy-start.5 = (bf16[16,16,1792]{2,1,0:T(8,128)(2,1)}, bf16[16,16,1792]{2,1,0:T(8,128)(2,1)S(1)}, u32[]{:S(2)}) copy-start(bf16[16,16,1792]{2,1,0:T(8,128)(2,1)S(1)} %all-to-all-done) | copy-start | bytes 2752516
  34.3 26.2 %all-to-all-start.2 = ((bf16[16,16,1792]{2,1,0:T(8,128)(2,1)}), bf16[16,16,1792]{2,1,0:T(8,128)(2,1)S(1)}, u32[]{:S(2)}, u32[]{:S(2)}) async-start(bf16[16,16,1792]{2,1,0:T(8,128)(2,1)} %bitcast.10), calls=%async_computation.2 | async-start | bytes 1835008 | tf_op jit(solution)/shard_map/all_to_all | solution.py:315
  39.8 10.0 %collective-permute-start = (bf16[256,1792]{1,0:T(8,128)(2,1)S(1)}, bf16[256,1792]{1,0:T(8,128)(2,1)S(1)}, u32[]{:S(2)}, u32[]{:S(2)}) collective-permute-start(bf16[256,1792]{1,0:T(8,128)(2,1)S(1)} %bitcast.23), channel_id=1, source_target_pairs={{0,1},{1,0},{2,3},{3,2},{4,5},{5,4},{6,7},{7,6},{8,9},{9,8},{10,11... | collective-permute-start | bytes 2752520 | tf_op jit(solution)/shard_map/ppermute | solution.py:310
  49.8 3.3 %copy-start = (bf16[1024,3584]{1,0:T(8,128)(2,1)}, bf16[1024,3584]{1,0:T(8,128)(2,1)S(1)}, u32[]{:S(2)}) copy-start(bf16[1024,3584]{1,0:T(8,128)(2,1)S(1)} %get-tuple-element.38.w_ref) | copy-start | bytes 22020100
  49.8 2.6 %copy-start.10 = (bf16[256,1792]{1,0:T(8,128)(2,1)}, bf16[256,1792]{1,0:T(8,128)(2,1)S(1)}, u32[]{:S(2)}) copy-start(bf16[256,1792]{1,0:T(8,128)(2,1)S(1)} %collective-permute-done.x_ref.oth_ref) | copy-start | bytes 2752516
  52.4 1.9 %copy-start.11 = (bf16[256,1024]{1,0:T(8,128)(2,1)}, bf16[256,1024]{1,0:T(8,128)(2,1)S(1)}, u32[]{:S(2)}) copy-start(bf16[256,1024]{1,0:T(8,128)(2,1)S(1)} %get-tuple-element.43.a_ref) | copy-start | bytes 1572868
  52.4 1.9 %copy-start.13 = (bf16[256,1024]{1,0:T(8,128)(2,1)}, bf16[256,1024]{1,0:T(8,128)(2,1)S(1)}, u32[]{:S(2)}) copy-start(bf16[256,1024]{1,0:T(8,128)(2,1)S(1)} %get-tuple-element.44.b_ref) | copy-start | bytes 1572868
  52.4 12.7 %copy-start.3 = (bf16[256,1024]{1,0:T(8,128)(2,1)}, bf16[256,1024]{1,0:T(8,128)(2,1)S(1)}, u32[]{:S(2)}) copy-start(bf16[256,1024]{1,0:T(8,128)(2,1)S(1)} %get-tuple-element.37.h_ref) | copy-start | bytes 1572868
  54.3 10.8 %collective-permute-start.1 = (bf16[256,1792]{1,0:T(8,128)(2,1)S(1)}, bf16[256,1792]{1,0:T(8,128)(2,1)}, u32[]{:S(2)}, u32[]{:S(2)}) collective-permute-start(bf16[256,1792]{1,0:T(8,128)(2,1)S(1)} %shard_map.133), channel_id=1, source_target_pairs={{0,1},{1,0},{2,3},{3,2},{4,5},{5,4},{6,7},{7,6},{8,9},{9,8},{10,11... | collective-permute-start | bytes 2752520 | tf_op jit(solution)/shard_map/ppermute | solution.py:310
  60.5 15.6 %copy-start.2 = (bf16[16,16,1792]{2,1,0:T(8,128)(2,1)}, bf16[16,16,1792]{2,1,0:T(8,128)(2,1)S(1)}, u32[]{:S(2)}) copy-start(bf16[16,16,1792]{2,1,0:T(8,128)(2,1)S(1)} %all-to-all-done.2) | copy-start | bytes 2752516
  60.5 21.0 %collective-permute-start.2 = (bf16[256,1792]{1,0:T(8,128)(2,1)S(1)}, bf16[256,1792]{1,0:T(8,128)(2,1)S(1)}, u32[]{:S(2)}, u32[]{:S(2)}) collective-permute-start(bf16[256,1792]{1,0:T(8,128)(2,1)S(1)} %bitcast.19), channel_id=1, source_target_pairs={{0,1},{1,0},{2,3},{3,2},{4,5},{5,4},{6,7},{7,6},{8,9},{9,8},{10,11... | collective-permute-start | bytes 2752520 | tf_op jit(solution)/shard_map/ppermute | solution.py:310
  60.5 3.4 %copy-start.1 = (bf16[1024,3584]{1,0:T(8,128)(2,1)S(1)}, bf16[1024,3584]{1,0:T(8,128)(2,1)}, u32[]{:S(2)}) copy-start(bf16[1024,3584]{1,0:T(8,128)(2,1)} %copy-done) | copy-start | bytes 22020100
  67.3 27.9 %all-to-all-start.1 = ((bf16[16,16,1792]{2,1,0:T(8,128)(2,1)}), bf16[16,16,1792]{2,1,0:T(8,128)(2,1)S(1)}, u32[]{:S(2)}, u32[]{:S(2)}) async-start(bf16[16,16,1792]{2,1,0:T(8,128)(2,1)} %bitcast.35), calls=%async_computation.1 | async-start | bytes 1835008 | tf_op jit(solution)/shard_map/all_to_all | solution.py:315
  76.1 5.4 %copy-start.12 = (bf16[256,1024]{1,0:T(8,128)(2,1)S(1)}, bf16[256,1024]{1,0:T(8,128)(2,1)}, u32[]{:S(2)}) copy-start(bf16[256,1024]{1,0:T(8,128)(2,1)} %copy-done.11) | copy-start | bytes 1572868
  76.1 5.4 %copy-start.14 = (bf16[256,1024]{1,0:T(8,128)(2,1)S(1)}, bf16[256,1024]{1,0:T(8,128)(2,1)}, u32[]{:S(2)}) copy-start(bf16[256,1024]{1,0:T(8,128)(2,1)} %copy-done.13) | copy-start | bytes 1572868
  81.5 3.4 %copy-start.4 = (bf16[256,1792]{1,0:T(8,128)(2,1)}, bf16[256,1792]{1,0:T(8,128)(2,1)S(1)}, u32[]{:S(2)}) copy-start(bf16[256,1792]{1,0:T(8,128)(2,1)S(1)} %collective-permute-done.2.dy_ref.oth_ref) | copy-start | bytes 2752516
  82.8 2.2 %copy-start.6 = (bf16[256,1024]{1,0:T(8,128)(2,1)}, bf16[256,1024]{1,0:T(8,128)(2,1)S(1)}, u32[]{:S(2)}) copy-start(bf16[256,1024]{1,0:T(8,128)(2,1)S(1)} %get-tuple-element.45.dg_ref) | copy-start | bytes 1572868
  82.8 2.2 %copy-start.7 = (bf16[256,1024]{1,0:T(8,128)(2,1)}, bf16[256,1024]{1,0:T(8,128)(2,1)S(1)}, u32[]{:S(2)}) copy-start(bf16[256,1024]{1,0:T(8,128)(2,1)S(1)} %get-tuple-element.46.du_ref) | copy-start | bytes 1572868
  84.9 2.5 %collective-permute-start.3 = (bf16[256,1792]{1,0:T(8,128)(2,1)S(1)}, bf16[256,1792]{1,0:T(8,128)(2,1)S(1)}, u32[]{:S(2)}, u32[]{:S(2)}) collective-permute-start(bf16[256,1792]{1,0:T(8,128)(2,1)S(1)} %shard_map.140), channel_id=1, source_target_pairs={{0,1},{1,0},{2,3},{3,2},{4,5},{5,4},{6,7},{7,6},{8,9},{9,8},{10,11... | collective-permute-start | bytes 2752520 | tf_op jit(solution)/shard_map/ppermute | solution.py:310
  95.2 14.4 %copy-start.20 = (bf16[16,16,1792]{2,1,0:T(8,128)(2,1)}, bf16[16,16,1792]{2,1,0:T(8,128)(2,1)S(1)}, u32[]{:S(2)}) copy-start(bf16[16,16,1792]{2,1,0:T(8,128)(2,1)S(1)} %all-to-all-done.1) | copy-start | bytes 2752516
  95.2 26.4 %all-to-all-start.3 = ((bf16[16,16,1792]{2,1,0:T(8,128)(2,1)}), bf16[16,16,1792]{2,1,0:T(8,128)(2,1)S(1)}, u32[]{:S(2)}, u32[]{:S(2)}) async-start(bf16[16,16,1792]{2,1,0:T(8,128)(2,1)} %bitcast.36), calls=%async_computation.3 | async-start | bytes 1835008 | tf_op jit(solution)/shard_map/all_to_all | solution.py:315
  100.8 8.9 %copy-start.9 = (bf16[256,1792]{1,0:T(8,128)(2,1)S(1)}, bf16[256,1792]{1,0:T(8,128)(2,1)}, u32[]{:S(2)}) copy-start(bf16[256,1792]{1,0:T(8,128)(2,1)} %out_ref.3) | copy-start | bytes 2752516
  100.8 8.9 %copy-start.16 = (f32[256,256]{1,0:T(8,128)S(1)}, f32[256,256]{1,0:T(8,128)}, u32[]{:S(2)}) copy-start(f32[256,256]{1,0:T(8,128)} %get-tuple-element.30.weight_ref) | copy-start | bytes 786436
  100.8 8.9 %copy-start.18 = (bf16[256,256]{1,0:T(8,128)(2,1)S(1)}, bf16[256,256]{1,0:T(8,128)(2,1)}, u32[]{:S(2)}) copy-start(bf16[256,256]{1,0:T(8,128)(2,1)} %get-tuple-element.29.pick_ref) | copy-start | bytes 393220
  100.8 8.9 %copy-start.19 = (s32[256,8]{0,1:T(8,128)S(1)}, s32[256,8]{0,1:T(8,128)}, u32[]{:S(2)}) copy-start(s32[256,8]{0,1:T(8,128)} %param.9) | copy-start | bytes 24580
  113.0 7.1 %collective-permute-start.4 = (f32[8,256]{1,0:T(8,128)S(1)}, f32[8,256]{1,0:T(8,128)S(1)}, u32[]{:S(2)}, u32[]{:S(2)}) collective-permute-start(f32[8,256]{1,0:T(8,128)S(1)} %get-tuple-element.49), channel_id=1, source_target_pairs={{0,1},{1,0},{2,3},{3,2},{4,5},{5,4},{6,7},{7,6},{8,9},{9,8},{10,11... | collective-permute-start | bytes 24584 | tf_op jit(solution)/shard_map/ppermute | solution.py:310
